TPU v7x, 128 devices: a whole 4x4x4 slice. The times are simulated.
128 devices in a mesh: space: 32 (over y_lo, z, x), vel: 4 (over y_hi, core).
Axes of the slice: x: 4, y: 4 (y_hi: 2, y_lo: 2; y = y_hi * 2 + y_lo), z: 4, core: 2. Of those that a mesh axis runs over, the one named last changes fastest.
Arguments:
- probe_field: float32 [2, 1024, 1024], P(None, 'space'), may hold values from -6 to 6
- control_field: float32 [2, 1024, 1024], P(None, 'space'), may hold values from -4 to 4
- optical_state: float32 [2, 64, 1024, 1024], P(None, 'vel', 'space'), may hold values from -3 to 3
- spin_state: float32 [2, 64, 1024, 1024], P(None, 'vel', 'space'), may hold values from -3 to 3
- doppler_shift: float32 [64], P('vel'), may hold values from -3 to 3
- class_weight: float32 [64], P('vel'), may hold values from 0.2 to 2
- gradient_shift: float32 [1024, 1024], P('space'), may hold values from -3 to 3
Outputs:
- probe_out: float32 [2, 1024, 1024], P(None, 'space')
- control_out: float32 [2, 1024, 1024], P(None, 'space')
- optical_out: float32 [2, 64, 1024, 1024], P(None, 'vel', 'space')
- spin_out: float32 [2, 64, 1024, 1024], P(None, 'vel', 'space')
All inputs are finite; a program needn't handle non-finite values.
Results may differ from a plain program's by a relative error of at most 0.000098.
Values sent between devices are 32-bit elements; how exact they have to be, the bound alone decides.
No kernel may reach another device: no remote copies, remote signals or barrier semaphores. Data moves between devices by JAX's collectives and lax.ppermute only.
A program may use at most 128 MiB of HBM per device.

v0:
```python
import jax
import jax.numpy as jnp
import numpy as np
from jax import lax
from jax.sharding import PartitionSpec as P

GRID = 1024
VEL = 64


GAMMA = 1.0
DEPHASE = 0.1
DT = 0.25
COUPLE = 2.0
HIGHEST = lax.Precision.HIGHEST


def in_order(tiles, dim):
    shape = list(tiles.shape[1:])
    shape[dim] *= tiles.shape[0]
    return jnp.moveaxis(tiles, 0, dim).reshape(shape)


def copy_for_each(shard, axis):
    devices = lax.axis_size(axis)
    return lax.all_to_all(
        jnp.broadcast_to(shard[None], (devices, *shard.shape)), axis, 0, 0, tiled=True
    )


def collect(shard, axis, dim):
    return in_order(copy_for_each(shard, axis), dim)


def cut_along(shard, dim, devices):
    shape = shard.shape
    tiles = shard.reshape(*shape[:dim], devices, shape[dim] // devices, *shape[dim + 1 :])
    return jnp.moveaxis(tiles, dim, 0)


def summed_on_arrival(shard, axis, dim):
    tiles = cut_along(shard, dim, lax.axis_size(axis))
    arrived = lax.all_to_all(tiles, axis, split_axis=0, concat_axis=0, tiled=True)
    return arrived.sum(axis=0)


def circulant_tables(grid_width):
    counter = np.arange(grid_width, dtype=np.int32)
    frequency = np.where(counter < grid_width // 2, counter, counter - grid_width)
    angles = (
        np.float32(np.pi)
        * (frequency * frequency % (2 * grid_width)).astype(np.float32)
        / np.float32(grid_width)
    )
    turns = counter[:, None] * counter[None, :] % grid_width
    argument = (
        np.float32(2.0 * np.pi) * turns.astype(np.float32) / np.float32(grid_width)
        - angles[None, :]
    )
    kernel_real = np.mean(np.cos(argument), axis=1)
    kernel_imag = np.mean(np.sin(argument), axis=1)
    offsets = (counter[:, None] - counter[None, :]) % grid_width
    return (kernel_real[offsets].astype(np.float32), kernel_imag[offsets].astype(np.float32))


def mix_left(table_real, table_imag, section):
    real_in, imag_in = (section[:, 0], section[:, 1])

    def product_of(table, values):
        return jnp.einsum("mn,fnk->fmk", table, values, precision=HIGHEST)

    return jnp.stack(
        [
            product_of(table_real, real_in) - product_of(table_imag, imag_in),
            product_of(table_real, imag_in) + product_of(table_imag, real_in),
        ],
        axis=1,
    )


def mix_right(section, table_real, table_imag):
    real_in, imag_in = (section[:, 0], section[:, 1])

    def product_of(values, table):
        return jnp.einsum("fmn,nk->fmk", values, table, precision=HIGHEST)

    return jnp.stack(
        [
            product_of(real_in, table_real) - product_of(imag_in, table_imag),
            product_of(imag_in, table_real) + product_of(real_in, table_imag),
        ],
        axis=1,
    )


def derivative(optical, spin_part, probe_part, control, doppler, gradient):
    optical_real, optical_imag = (optical[0], optical[1])
    spin_real, spin_imag = (spin_part[0], spin_part[1])
    probe_real, probe_imag = (probe_part[0], probe_part[1])
    control_real, control_imag = (control[0], control[1])
    rate_optical_real = (
        -GAMMA * optical_real
        + doppler * optical_imag
        - probe_imag
        - (control_real * spin_imag + control_imag * spin_real)
    )
    rate_optical_imag = (
        -GAMMA * optical_imag
        - doppler * optical_real
        + probe_real
        + (control_real * spin_real - control_imag * spin_imag)
    )
    rate_spin_real = (
        -DEPHASE * spin_real
        + gradient * spin_imag
        - (control_real * optical_imag - control_imag * optical_real)
    )
    rate_spin_imag = (
        -DEPHASE * spin_imag
        - gradient * spin_real
        + (control_real * optical_real + control_imag * optical_imag)
    )
    return (
        jnp.stack([rate_optical_real, rate_optical_imag]),
        jnp.stack([rate_spin_real, rate_spin_imag]),
    )


def midpoint(optical, spin_part, probe_part, control, doppler, gradient):
    rate_optical, rate_spin = derivative(optical, spin_part, probe_part, control, doppler, gradient)
    half_optical = optical + 0.5 * DT * rate_optical
    half_spin = spin_part + 0.5 * DT * rate_spin
    rate_optical, rate_spin = derivative(
        half_optical, half_spin, probe_part, control, doppler, gradient
    )
    return (optical + DT * rate_optical, spin_part + DT * rate_spin)


def add_source(complex_field, polarization):
    return jnp.stack(
        [complex_field[0] - COUPLE * polarization[1], complex_field[1] + COUPLE * polarization[0]]
    )


def shards(
    probe_field,
    control_field,
    optical_state,
    spin_state,
    doppler_shift,
    class_weight,
    gradient_shift,
):
    grid_width = GRID
    quarter_width = grid_width // lax.axis_size("vel")
    table_real, table_imag = circulant_tables(grid_width)
    full_real = jnp.asarray(table_real)
    full_imag = jnp.asarray(table_imag)

    def row_mix(section):
        blended = mix_left(
            full_real,
            full_imag,
            lax.all_to_all(section, "space", split_axis=3, concat_axis=2, tiled=True),
        )
        return lax.all_to_all(blended, "space", split_axis=2, concat_axis=3, tiled=True)

    def spread(section):
        return collect(section, "vel", 3)

    stacked = jnp.stack([probe_field, control_field])
    col_start = lax.axis_index("vel") * quarter_width
    quart_real = lax.dynamic_slice_in_dim(full_real, col_start, quarter_width, 1)
    quart_imag = lax.dynamic_slice_in_dim(full_imag, col_start, quarter_width, 1)
    stacked = spread(row_mix(mix_right(stacked, quart_real, quart_imag)))
    optical_new, spin_new = midpoint(
        optical_state,
        spin_state,
        stacked[0],
        stacked[1],
        doppler_shift[:, None, None],
        gradient_shift,
    )
    weighted = jnp.einsum("cvrn,v->crn", optical_new, class_weight, precision=HIGHEST) / VEL
    polarization = summed_on_arrival(weighted, "vel", 2)
    probe_part = lax.dynamic_slice_in_dim(stacked[0], col_start, quarter_width, 2)
    control_part = lax.dynamic_slice_in_dim(stacked[1], col_start, quarter_width, 2)
    section = jnp.stack([add_source(probe_part, polarization), control_part])
    stacked = mix_right(spread(row_mix(section)), full_real, full_imag)
    return (stacked[0], stacked[1], optical_new, spin_new)


def solution(mesh):
    return jax.shard_map(
        shards,
        mesh=mesh,
        in_specs=(
            P(None, "space", None),
            P(None, "space", None),
            P(None, "vel", "space", None),
            P(None, "vel", "space", None),
            P("vel"),
            P("vel"),
            P("space", None),
        ),
        out_specs=(
            P(None, "space", None),
            P(None, "space", None),
            P(None, "vel", "space", None),
            P(None, "vel", "space", None),
        ),
        check_vma=False,
    )
```

profile of v0, /device:TPU:1, one launch (start us, length us, event | category | flops | bytes accessed | tf_op | source)
XLA Modules:
  0.0 201.8 jit_solution(2119984255161976358)
XLA Ops:
  0.7 2.0 %fusion.18 = f32[2,32,256]{2,1,0:T(8,128)S(1)} fusion(f32[1024,1024]{1,0:T(8,128)} %constant.29.clone, s32[]{:T(128)S(6)} %select_n.2, f32[1,2,32,1024]{3,2,0,1:T(8,128)} %bitcast.158, f32[1,2,32,1024]{3,2,0,1:T(8,128)} %bitcast.162), kind=kOutput, calls=%fused_computation.38 | convolution fusion | flops 201392128 | bytes 1638404 | tf_op jit(solution)/shard_map/fmn,nk->fmk/dot_general | solution.py:85
  2.7 2.0 fusion.20
  4.7 1.9 fusion.12
  6.6 1.9 fusion.13
  8.5 0.3 copy.37
  8.8 0.5 reshape.41
  9.4 16.8 %all_to_all.81 = f32[32,1,1024]{2,1,0:T(1,128)S(1)} all-to-all(f32[32,1,1024]{2,1,0:T(1,128)S(1)} %reshape.41), channel_id=1, replica_groups=mesh['space'=32,'vel'=4] {'space'}, dimensions={0} | all-to-all | bytes 262144 | tf_op jit(solution)/shard_map/all_to_all | solution.py:164
  26.2 0.5 broadcast.75
  26.7 1.0 reduce
  27.7 0.4 reshape.42
  28.3 0.2 all_to_all.60
  28.5 5.8 %fusion.35 = f32[2,8,1024]{2,1,0:T(8,128)S(1)} fusion(f32[1024,1024,1]{1,0,2:T(8,128)} %constant.31, f32[2,2,1024,8]{2,3,0,1:T(8,128)S(1)} %all_to_all.60), kind=kOutput, calls=%fused_computation.74 | convolution fusion | flops 201326592 | bytes 4325376 | tf_op jit(solution)/shard_map/mn,fnk->fmk/dot_general | solution.py:70
  34.4 3.5 %fusion.34 = f32[2,8,1024]{2,1,0:T(8,128)S(1)} fusion(f32[1024,1024,1]{1,0,2:T(8,128)S(1)} %copy-done.5, f32[2,2,1024,8]{2,3,0,1:T(8,128)S(1)} %all_to_all.60), kind=kOutput, calls=%fused_computation.73 | convolution fusion | flops 201326592 | bytes 4325376 | tf_op jit(solution)/shard_map/mn,fnk->fmk/dot_general | solution.py:70
  37.9 3.5 %fusion.10 = f32[2,1,1024,8]{2,3,0,1:T(8,128)S(1)} fusion(f32[2,8,1024]{2,1,0:T(8,128)S(1)} %fusion.35, f32[1024,1024,1]{1,0,2:T(8,128)S(1)} %copy-done.2, f32[2,2,1024,8]{2,3,0,1:T(8,128)S(1)} %all_to_all.60), kind=kOutput, calls=%fused_computation.27 | convolution fusion | flops 201342976 | bytes 4390912 | tf_op jit(solution)/shard_map/mn,fnk->fmk/dot_general | solution.py:70
  41.4 3.9 %fusion.11 = f32[2,1,1024,8]{2,3,0,1:T(8,128)S(1)} fusion(f32[2,8,1024]{2,1,0:T(8,128)S(1)} %fusion.34, f32[1024,1024,1]{1,0,2:T(8,128)S(1)} %copy-done.2, f32[2,2,1024,8]{2,3,0,1:T(8,128)S(1)} %all_to_all.60), kind=kOutput, calls=%fused_computation.29 | convolution fusion | flops 201342976 | bytes 4390912 | tf_op jit(solution)/shard_map/mn,fnk->fmk/dot_general | solution.py:70
  45.4 1.3 copy.40
  46.8 3.3 %reshape.43 = f32[32,1,1024]{2,1,0:T(1,128)S(1)} reshape(f32[1024,2,2,8]{3,2,1,0:T(2,128)S(1)} %bitcast.150) | data formatting | bytes 262144
  50.1 10.9 %all_to_all.82 = f32[32,1,1024]{2,1,0:T(1,128)S(1)} all-to-all(f32[32,1,1024]{2,1,0:T(1,128)S(1)} %reshape.43), channel_id=1, replica_groups=mesh['space'=32,'vel'=4] {'space'}, dimensions={0} | all-to-all | bytes 262144 | tf_op jit(solution)/shard_map/all_to_all | solution.py:166
  60.9 1.0 reduce.1
  61.9 3.2 %reshape.44 = f32[1024,2,2,8]{3,2,1,0:T(2,128)S(1)} reshape(f32[32,1024]{1,0:T(8,128)S(1)} %reduce.1) | data formatting | bytes 262144
  65.1 1.8 copy.41
  67.0 0.9 broadcast_in_dim.9
  67.9 7.7 %all-to-all-start.2 = ((f32[4,2,2,32,256]{4,3,2,1,0:T(8,128)}), f32[4,2,2,32,256]{4,3,2,1,0:T(8,128)S(1)}, u32[]{:S(2)}, u32[]{:S(2)}) async-start(f32[4,2,2,32,256]{4,3,2,1,0:T(8,128)} %broadcast_in_dim.9), calls=%async_computation.2 | async-start | bytes 1048576 | tf_op jit(solution)/shard_map/all_to_all | solution.py:26
  75.6 9.3 %all-to-all-done.2 = f32[4,2,2,32,256]{4,3,2,1,0:T(8,128)S(1)} async-done(((f32[4,2,2,32,256]{4,3,2,1,0:T(8,128)}), f32[4,2,2,32,256]{4,3,2,1,0:T(8,128)S(1)}, u32[]{:S(2)}, u32[]{:S(2)}) %all-to-all-start.2) | async-done | bytes 524320 | tf_op jit(solution)/shard_map/all_to_all | solution.py:26
  85.6 4.8 %subtract_subtract_fusion.1 = (f32[1,16,32,1024]{3,2,1,0:T(8,128)S(1)}, f32[1,16,32,1024]{3,2,1,0:T(8,128)S(1)}) fusion(f32[2,16,32,1024]{3,2,1,0:T(8,128)} %param.12, f32[2,16,32,1024]{3,2,1,0:T(8,128)} %param.11, f32[32,1024]{1,0:T(8,128)S(1)} %copy-done.16, f32[32,1024]{1,0:T(8,128)S(1)} %bitcast.166, f32[32,1024]{1,0:T(8,128)S(1)} %bitcast.170), kind=kLoop, calls=%fused_computation.15 | loop fusion | flops 7340032 | bytes 12976128 | tf_op jit(solution)/shard_map/sub | solution.py:114
  90.3 1.1 copy-done.9
  91.5 1.6 add_subtract_fusion.1
  93.1 2.9 %fusion = (f32[2,16,32,1024]{3,2,1,0:T(8,128)S(1)}, f32[2,16,32,1024]{3,2,1,0:T(8,128)S(1)}) fusion(f32[2,16,32,1024]{3,2,1,0:T(8,128)S(1)} %copy-done.8, f32[1,16,32,1024]{3,2,1,0:T(8,128)S(1)} %get-tuple-element.11, f32[1,16,32,1024]{3,2,1,0:T(8,128)S(1)} %get-tuple-element.10, f32[2,16,32,1024]{3,2,1,0:T(8,128)S(1)} %copy-done.9, ...), kind=kLoop, calls=%fused_computation.1 | loop fusion | flops 6291456 | bytes 25165824 | tf_op jit(solution)/shard_map/add | solution.py:131
  96.0 1.7 add_subtract_fusion
  97.7 1.3 copy-done.11
  99.0 0.4 copy-done.12
  99.4 1.4 fusion.2
  100.9 4.7 %fusion.4 = f32[1,2,32,1024]{3,0,2,1:T(1,128)S(1)} fusion(f32[2,16,32,1024]{3,2,1,0:T(8,128)S(1)} %fusion.2, f32[16]{0:T(128)S(1)} %copy-done), kind=kOutput, calls=%fused_computation.8 | convolution fusion | flops 12582912 | bytes 4456512 | tf_op jit(solution)/shard_map/cvrn,v->crn/dot_general | solution.py:184
  105.7 0.8 copy.48
  106.5 4.3 %all-to-all-start.3 = ((f32[4,2,32,256]{3,2,1,0:T(8,128)}), f32[4,2,32,256]{3,2,1,0:T(8,128)S(1)}, u32[]{:S(2)}, u32[]{:S(2)}) async-start(f32[4,2,32,256]{3,2,1,0:T(8,128)} %copy.48), calls=%async_computation.3 | async-start | bytes 524288 | tf_op jit(solution)/shard_map/all_to_all | solution.py:43
  110.9 0.2 copy.49
  111.6 5.8 %all-to-all-done.3 = f32[4,2,32,256]{3,2,1,0:T(8,128)S(1)} async-done(((f32[4,2,32,256]{3,2,1,0:T(8,128)}), f32[4,2,32,256]{3,2,1,0:T(8,128)S(1)}, u32[]{:S(2)}, u32[]{:S(2)}) %all-to-all-start.3) | async-done | bytes 262176 | tf_op jit(solution)/shard_map/all_to_all | solution.py:43
  117.5 0.3 copy.50
  117.8 0.5 reshape.45
  118.3 10.7 %all_to_all.83 = f32[32,1,1024]{2,1,0:T(1,128)S(1)} all-to-all(f32[32,1,1024]{2,1,0:T(1,128)S(1)} %reshape.45), channel_id=1, replica_groups=mesh['space'=32,'vel'=4] {'space'}, dimensions={0} | all-to-all | bytes 262144 | tf_op jit(solution)/shard_map/all_to_all | solution.py:164
  129.0 1.0 reduce.2
  130.0 0.4 reshape.46
  130.6 0.2 all_to_all.69
  130.9 5.8 %fusion.37 = f32[2,8,1024]{2,1,0:T(8,128)S(1)} fusion(f32[1024,1024,1]{1,0,2:T(8,128)} %constant.31, f32[2,2,1024,8]{2,3,0,1:T(8,128)S(1)} %all_to_all.69), kind=kOutput, calls=%fused_computation.76 | convolution fusion | flops 201326592 | bytes 4325376 | tf_op jit(solution)/shard_map/mn,fnk->fmk/dot_general | solution.py:70
  136.7 3.5 %fusion.36 = f32[2,8,1024]{2,1,0:T(8,128)S(1)} fusion(f32[1024,1024,1]{1,0,2:T(8,128)S(1)} %copy-done.6, f32[2,2,1024,8]{2,3,0,1:T(8,128)S(1)} %all_to_all.69), kind=kOutput, calls=%fused_computation.75 | convolution fusion | flops 201326592 | bytes 4325376 | tf_op jit(solution)/shard_map/mn,fnk->fmk/dot_general | solution.py:70
  140.2 3.5 %fusion.8 = f32[2,1,1024,8]{2,3,0,1:T(8,128)S(1)} fusion(f32[2,8,1024]{2,1,0:T(8,128)S(1)} %fusion.37, f32[1024,1024,1]{1,0,2:T(8,128)S(1)} %copy-done.3, f32[2,2,1024,8]{2,3,0,1:T(8,128)S(1)} %all_to_all.69), kind=kOutput, calls=%fused_computation.23 | convolution fusion | flops 201342976 | bytes 4390912 | tf_op jit(solution)/shard_map/mn,fnk->fmk/dot_general | solution.py:70
  143.8 3.7 %fusion.9 = f32[2,1,1024,8]{2,3,0,1:T(8,128)S(1)} fusion(f32[2,8,1024]{2,1,0:T(8,128)S(1)} %fusion.36, f32[1024,1024,1]{1,0,2:T(8,128)S(1)} %copy-done.3, f32[2,2,1024,8]{2,3,0,1:T(8,128)S(1)} %all_to_all.69), kind=kOutput, calls=%fused_computation.25 | convolution fusion | flops 201342976 | bytes 4390912 | tf_op jit(solution)/shard_map/mn,fnk->fmk/dot_general | solution.py:70
  147.6 1.3 copy.53
  148.9 4.0 %reshape.47 = f32[32,1,1024]{2,1,0:T(1,128)} reshape(f32[1024,2,2,8]{3,2,1,0:T(2,128)S(1)} %bitcast.151) | data formatting | bytes 262144
  152.9 3.9 %all-to-all-start.5 = ((f32[32,1,1024]{2,1,0:T(1,128)}), f32[32,1,1024]{2,1,0:T(1,128)S(1)}, u32[]{:S(2)}, u32[]{:S(2)}) async-start(f32[32,1,1024]{2,1,0:T(1,128)} %reshape.47), calls=%async_computation.5 | async-start | bytes 262144 | tf_op jit(solution)/shard_map/all_to_all | solution.py:166
  156.8 7.0 %subtract_subtract_fusion = (f32[1,16,32,1024]{3,2,1,0:T(8,128)}, f32[1,16,32,1024]{3,2,1,0:T(8,128)}) fusion(f32[2,16,32,1024]{3,2,1,0:T(8,128)} %copy-done.12, f32[2,16,32,1024]{3,2,1,0:T(8,128)} %copy-done.11, f32[32,1024]{1,0:T(8,128)S(1)} %copy-done.16, f32[32,1024]{1,0:T(8,128)S(1)} %bitcast.169, f32[32,1024]{1,0:T(8,128)S(1)} %bitcast.173), kind=kLoop, calls=%fused_computation.11 | loop fusion | flops 7340032 | bytes 12976128 | tf_op jit(solution)/shard_map/sub | solution.py:114
  163.7 0.3 all-to-all-done.5
  164.1 1.0 reduce.3
  165.0 3.2 %reshape.48 = f32[1024,2,2,8]{3,2,1,0:T(2,128)S(1)} reshape(f32[32,1024]{1,0:T(8,128)S(1)} %reduce.3) | data formatting | bytes 262144
  168.2 1.8 copy.54
  170.2 0.9 broadcast_in_dim.11
  171.0 7.3 %all-to-all-start.6 = ((f32[4,2,2,32,256]{4,3,1,2,0:T(8,128)}), f32[4,2,2,32,256]{4,3,1,2,0:T(8,128)S(1)}, u32[]{:S(2)}, u32[]{:S(2)}) async-start(f32[4,2,2,32,256]{4,3,1,2,0:T(8,128)} %broadcast_in_dim.11), calls=%async_computation.6 | async-start | bytes 1048576 | tf_op jit(solution)/shard_map/all_to_all | solution.py:26
  178.3 6.1 %fusion.3 = f32[2,16,32,1024]{3,2,1,0:T(8,128)} fusion(f32[2,16,32,1024]{3,2,1,0:T(8,128)} %param.12, f32[1,16,32,1024]{3,2,1,0:T(8,128)} %get-tuple-element.5, f32[1,16,32,1024]{3,2,1,0:T(8,128)S(1)} %copy-done.13), kind=kLoop, calls=%fused_computation.7 | loop fusion | flops 3145728 | bytes 12582912 | tf_op jit(solution)/shard_map/add | solution.py:136
  184.4 3.2 %all-to-all-done.6 = f32[4,2,2,32,256]{4,3,1,2,0:T(8,128)S(1)} async-done(((f32[4,2,2,32,256]{4,3,1,2,0:T(8,128)}), f32[4,2,2,32,256]{4,3,1,2,0:T(8,128)S(1)}, u32[]{:S(2)}, u32[]{:S(2)}) %all-to-all-start.6) | async-done | bytes 524320 | tf_op jit(solution)/shard_map/all_to_all | solution.py:26
  187.7 5.0 %fusion.31 = f32[2,32,1024]{2,1,0:T(8,128)S(1)} fusion(f32[1024,1024,1]{1,0,2:T(8,128)} %constant.31, f32[2,2,32,1024]{3,2,0,1:T(8,128)S(1)} %bitcast.152), kind=kOutput, calls=%fused_computation.62 | convolution fusion | flops 805306368 | bytes 4718592 | tf_op jit(solution)/shard_map/fmn,nk->fmk/dot_general | solution.py:85
  192.7 2.6 %fusion.30 = f32[2,32,1024]{2,1,0:T(8,128)S(1)} fusion(f32[1024,1024,1]{1,0,2:T(8,128)S(1)} %copy-done.7, f32[2,2,32,1024]{3,2,0,1:T(8,128)S(1)} %bitcast.153), kind=kOutput, calls=%fused_computation.61 | convolution fusion | flops 805306368 | bytes 4718592 | tf_op jit(solution)/shard_map/fmn,nk->fmk/dot_general | solution.py:85
  195.4 2.6 %fusion.6 = f32[2,1,32,1024]{3,2,0,1:T(8,128)S(1)} fusion(f32[2,32,1024]{2,1,0:T(8,128)S(1)} %fusion.31, f32[1024,1024,1]{1,0,2:T(8,128)S(1)} %copy-done.4, f32[2,2,32,1024]{3,2,0,1:T(8,128)S(1)} %bitcast.154), kind=kOutput, calls=%fused_computation.19 | convolution fusion | flops 805371904 | bytes 4980736 | tf_op jit(solution)/shard_map/fmn,nk->fmk/dot_general | solution.py:85
  198.0 2.6 %fusion.7 = f32[2,1,32,1024]{3,2,0,1:T(8,128)S(1)} fusion(f32[2,32,1024]{2,1,0:T(8,128)S(1)} %fusion.30, f32[1024,1024,1]{1,0,2:T(8,128)S(1)} %copy-done.4, f32[2,2,32,1024]{3,2,0,1:T(8,128)S(1)} %bitcast.155), kind=kOutput, calls=%fused_computation.21 | convolution fusion | flops 805371904 | bytes 4980736 | tf_op jit(solution)/shard_map/fmn,nk->fmk/dot_general | solution.py:85
  200.7 0.8 fusion.28
  (63 shorter events, 2.0 us)
Async XLA Ops:
  0.6 100.2 %copy-start = (f32[16]{0:T(128)S(1)}, f32[16]{0:T(128)}, u32[]{:S(2)}) copy-start(f32[16]{0:T(128)} %param.14) | copy-start | bytes 196
  0.6 4.1 %copy-start.14 = (f32[2,32,1024]{2,1,0:T(8,128)S(1)}, f32[2,32,1024]{2,1,0:T(8,128)}, u32[]{:S(2)}) copy-start(f32[2,32,1024]{2,1,0:T(8,128)} %param.10) | copy-start | bytes 786436
  0.7 4.1 %copy-start.15 = (f32[2,32,1024]{2,1,0:T(8,128)S(1)}, f32[2,32,1024]{2,1,0:T(8,128)}, u32[]{:S(2)}) copy-start(f32[2,32,1024]{2,1,0:T(8,128)} %param.9) | copy-start | bytes 786436
  28.5 5.8 %copy-start.5 = (f32[1024,1024,1]{1,0,2:T(8,128)S(1)}, f32[1024,1024,1]{1,0,2:T(8,128)}, u32[]{:S(2)}) copy-start(f32[1024,1024,1]{1,0,2:T(8,128)} %constant.31) | copy-start | bytes 12582916
  34.4 3.5 %copy-start.2 = (f32[1024,1024,1]{1,0,2:T(8,128)S(1)}, f32[1024,1024,1]{1,0,2:T(8,128)}, u32[]{:S(2)}) copy-start(f32[1024,1024,1]{1,0,2:T(8,128)} %constant.32) | copy-start | bytes 12582916
  67.9 17.6 %copy-start.16 = (f32[32,1024]{1,0:T(8,128)S(1)}, f32[32,1024]{1,0:T(8,128)}, u32[]{:S(2)}) copy-start(f32[32,1024]{1,0:T(8,128)} %param.15) | copy-start | bytes 393220
  67.9 17.1 %all-to-all-start.2 = ((f32[4,2,2,32,256]{4,3,2,1,0:T(8,128)}), f32[4,2,2,32,256]{4,3,2,1,0:T(8,128)S(1)}, u32[]{:S(2)}, u32[]{:S(2)}) async-start(f32[4,2,2,32,256]{4,3,2,1,0:T(8,128)} %broadcast_in_dim.9), calls=%async_computation.2 | async-start | bytes 1048576 | tf_op jit(solution)/shard_map/all_to_all | solution.py:26
  85.5 4.8 %copy-start.8 = (f32[2,16,32,1024]{3,2,1,0:T(8,128)S(1)}, f32[2,16,32,1024]{3,2,1,0:T(8,128)}, u32[]{:S(2)}) copy-start(f32[2,16,32,1024]{3,2,1,0:T(8,128)} %param.11) | copy-start | bytes 12582916
  85.5 5.9 %copy-start.9 = (f32[2,16,32,1024]{3,2,1,0:T(8,128)S(1)}, f32[2,16,32,1024]{3,2,1,0:T(8,128)}, u32[]{:S(2)}) copy-start(f32[2,16,32,1024]{3,2,1,0:T(8,128)} %param.12) | copy-start | bytes 12582916
  85.5 5.9 %copy-start.17 = (f32[16]{0:T(128)S(1)}, f32[16]{0:T(128)}, u32[]{:S(2)}) copy-start(f32[16]{0:T(128)} %param.13) | copy-start | bytes 196
  96.0 3.0 %copy-start.11 = (f32[2,16,32,1024]{3,2,1,0:T(8,128)}, f32[2,16,32,1024]{3,2,1,0:T(8,128)S(1)}, u32[]{:S(2)}) copy-start(f32[2,16,32,1024]{3,2,1,0:T(8,128)S(1)} %get-tuple-element.22) | copy-start | bytes 12582916
  96.0 3.4 %copy-start.12 = (f32[2,16,32,1024]{3,2,1,0:T(8,128)}, f32[2,16,32,1024]{3,2,1,0:T(8,128)S(1)}, u32[]{:S(2)}) copy-start(f32[2,16,32,1024]{3,2,1,0:T(8,128)S(1)} %get-tuple-element.23) | copy-start | bytes 12582916
  100.8 4.7 %copy-start.10 = (f32[2,16,32,1024]{3,2,1,0:T(8,128)}, f32[2,16,32,1024]{3,2,1,0:T(8,128)S(1)}, u32[]{:S(2)}) copy-start(f32[2,16,32,1024]{3,2,1,0:T(8,128)S(1)} %fusion.2) | copy-start | bytes 12582916
  106.5 10.9 %all-to-all-start.3 = ((f32[4,2,32,256]{3,2,1,0:T(8,128)}), f32[4,2,32,256]{3,2,1,0:T(8,128)S(1)}, u32[]{:S(2)}, u32[]{:S(2)}) async-start(f32[4,2,32,256]{3,2,1,0:T(8,128)} %copy.48), calls=%async_computation.3 | async-start | bytes 524288 | tf_op jit(solution)/shard_map/all_to_all | solution.py:43
  130.8 5.8 %copy-start.6 = (f32[1024,1024,1]{1,0,2:T(8,128)S(1)}, f32[1024,1024,1]{1,0,2:T(8,128)}, u32[]{:S(2)}) copy-start(f32[1024,1024,1]{1,0,2:T(8,128)} %constant.31) | copy-start | bytes 12582916
  136.7 3.5 %copy-start.3 = (f32[1024,1024,1]{1,0,2:T(8,128)S(1)}, f32[1024,1024,1]{1,0,2:T(8,128)}, u32[]{:S(2)}) copy-start(f32[1024,1024,1]{1,0,2:T(8,128)} %constant.32) | copy-start | bytes 12582916
  152.9 11.2 %all-to-all-start.5 = ((f32[32,1,1024]{2,1,0:T(1,128)}), f32[32,1,1024]{2,1,0:T(1,128)S(1)}, u32[]{:S(2)}, u32[]{:S(2)}) async-start(f32[32,1,1024]{2,1,0:T(1,128)} %reshape.47), calls=%async_computation.5 | async-start | bytes 262144 | tf_op jit(solution)/shard_map/all_to_all | solution.py:166
  170.0 8.3 %copy-start.13 = (f32[1,16,32,1024]{3,2,1,0:T(8,128)S(1)}, f32[1,16,32,1024]{3,2,1,0:T(8,128)}, u32[]{:S(2)}) copy-start(f32[1,16,32,1024]{3,2,1,0:T(8,128)} %get-tuple-element.4) | copy-start | bytes 6291460
  171.0 16.6 %all-to-all-start.6 = ((f32[4,2,2,32,256]{4,3,1,2,0:T(8,128)}), f32[4,2,2,32,256]{4,3,1,2,0:T(8,128)S(1)}, u32[]{:S(2)}, u32[]{:S(2)}) async-start(f32[4,2,2,32,256]{4,3,1,2,0:T(8,128)} %broadcast_in_dim.11), calls=%async_computation.6 | async-start | bytes 1048576 | tf_op jit(solution)/shard_map/all_to_all | solution.py:26
  187.7 5.0 %copy-start.7 = (f32[1024,1024,1]{1,0,2:T(8,128)S(1)}, f32[1024,1024,1]{1,0,2:T(8,128)}, u32[]{:S(2)}) copy-start(f32[1024,1024,1]{1,0,2:T(8,128)} %constant.31) | copy-start | bytes 12582916
  192.7 2.7 %copy-start.4 = (f32[1024,1024,1]{1,0,2:T(8,128)S(1)}, f32[1024,1024,1]{1,0,2:T(8,128)}, u32[]{:S(2)}) copy-start(f32[1024,1024,1]{1,0,2:T(8,128)} %constant.32) | copy-start | bytes 12582916
  195.4 6.1 %copy-start.1 = (f32[16]{0:T(128)S(1)}, f32[16]{0:T(128)}, u32[]{:S(2)}) copy-start(f32[16]{0:T(128)} %param.14) | copy-start | bytes 196
where the time goes:
time: 205 us; the launch traced here: 202 us
  matrix products  58.8 us (29%)
  blocking collectives  38.4 us (19%)
  local copies, waits for them, and re-layouts  30.8 us (15%)
  other arithmetic  30.2 us (15%)
  starting transfers between devices  23.2 us (11%)
  waiting for transfers between devices  18.7 us (9%)
    dot_general x8, matrix products, product_of(): return jnp.einsum('mn,fnk->fmk', table, values, precision=HIGHEST)  33.4 us
    all_to_all x2, blocking collectives, row_mix(): lax.all_to_all(section, 'space', split_axis=3, concat_axis=2, tiled=True)  27.5 us
    dot_general x8, matrix products, product_of(): return jnp.einsum('fmn,nk->fmk', values, table, precision=HIGHEST)  20.7 us
    unnamed x48, local copies, waits for them, and re-layouts  18.7 us
    all_to_all x2, starting transfers between devices, copy_for_each(): lax.all_to_all(jnp.broadcast_to(shard[None], (devices, *shard.shape)), ax...  15 us
    all_to_all x2, waiting for transfers between devices, copy_for_each(): lax.all_to_all(jnp.broadcast_to(shard[None], (devices, *shard.shape)), ax...  12.6 us
    sub x2, other arithmetic, derivative(): -DEPHASE * spin_real + gradient * spin_imag  11.7 us
    all_to_all x1, blocking collectives, row_mix(): lax.all_to_all(blended, 'space', split_axis=2, concat_axis=3, tiled=True)  10.9 us
  transfers between devices with their start and end apart: 4, of which 4 were waited for; matrix products, arithmetic and copies ran while one was open for 7% of the time, Pallas kernels for 0%

commit v1 on v0

v1 whole, which is shorter than its diff:
```python
import jax
import jax.numpy as jnp
import numpy as np
from jax import lax
from jax.experimental import pallas as pl
from jax.experimental.pallas import tpu as pltpu
from jax.sharding import Mesh
from jax.sharding import PartitionSpec as P


N = 1024
BF16 = jnp.bfloat16
F32 = jnp.float32


def turn(numerator, period):
    angle = 2.0 * np.pi * (np.asarray(numerator, np.int64) % period) / period
    return np.cos(angle) + 1j * np.sin(angle)


NORM = np.exp(-0.25j * np.pi) / 32.0


def chirp(n):
    return turn(np.asarray(n, np.int64) ** 2, 2 * N)


def pair(z):
    return np.stack([z.real, z.imag]).astype(np.float32)


def halves(x):
    x = np.asarray(x, np.float32)
    high = x.astype(BF16)
    low = (x - high.astype(np.float32)).astype(BF16)
    return np.stack([high, low])


def row_tables():
    n = np.arange(N)
    pre = pair(NORM * chirp(n))
    short = np.arange(256)
    twiddle = pair(turn(-np.arange(4)[:, None] * short[None, :], N)).reshape(8, 256)
    dft = turn(-np.arange(128)[:, None] * short[None, :], 256)
    table = halves(np.concatenate([dft.real, dft.imag], axis=0))
    out = 4 * np.arange(128)[:, None] + np.repeat(np.arange(4), 32)[None, :]
    return pre, twiddle, table, pair(chirp(out))


def column_tables():
    eye = np.eye(4)
    small = turn(-np.arange(32)[:, None] * np.arange(32)[None, :], 32)
    right = np.concatenate([np.kron(eye, small.real), np.kron(eye, small.imag)], axis=1)
    inner = np.tile(np.arange(32), 4)
    twiddle = pair(turn(-inner[:, None] * inner[None, :], N))
    wave = chirp(32 * inner[:, None] + inner[None, :])
    return halves(right), halves(right.T), twiddle, pair(wave), pair(NORM * wave)


def last_tables():
    c2, h, c1, t = np.meshgrid(np.arange(2), np.arange(2), np.arange(4), np.arange(16), indexing="ij")
    quarter = (128 * h + 16 * (2 * c1 + c2) + t).reshape(-1)
    classes = np.arange(4)
    pre = pair(NORM * chirp(4 * quarter[None, :] + classes[:, None])).reshape(8, 256)
    short = np.arange(256)
    dft = turn(-quarter[:, None] * short[None, :], 256)
    table = halves(np.concatenate([dft.real, dft.imag], axis=1))
    twiddle = pair(turn(-classes[:, None] * short[None, :], N)).reshape(8, 256)
    return pre, table, twiddle, pair(chirp(np.arange(N)))


def split(x):
    high = x.astype(BF16)
    return high, (x - high.astype(F32)).astype(BF16)


def mm(a, b, dims):
    return lax.dot_general(a, b, (dims, ((), ())), preferred_element_type=F32)


def mm3(a, b, dims):
    (ah, al), (bh, bl) = a, b
    return mm(ah, bh, dims) + (mm(ah, bl, dims) + mm(al, bh, dims))


def cmul(xr, xi, yr, yi):
    return xr * yr - xi * yi, xr * yi + xi * yr


def butterfly(r, i):
    ar, ai, br, bi = r[0] + r[2], i[0] + i[2], r[0] - r[2], i[0] - i[2]
    cr, ci, dr, di = r[1] + r[3], i[1] + i[3], r[1] - r[3], i[1] - i[3]
    return (
        [ar + cr, br + di, ar - cr, br - di],
        [ai + ci, bi - dr, ai - ci, bi + dr],
    )


def rows_kernel(probe, control, pre, twiddle, table, post, out):
    core, half = lax.axis_index("co"), lax.axis_index("yh")
    first = half == 0
    xr = jnp.where(first, probe[0], control[0])
    xi = jnp.where(first, probe[1], control[1])
    lane = lax.broadcasted_iota(jnp.int32, (1, N), 1)
    sign = jnp.where((lane & core) == 1, -1.0, 1.0)
    xr, xi = cmul(xr, xi, pre[0:1, :] * sign, pre[1:2, :] * sign)
    r, i = butterfly(
        [xr[:, 256 * k : 256 * k + 256] for k in range(4)],
        [xi[:, 256 * k : 256 * k + 256] for k in range(4)],
    )
    for p in range(1, 4):
        r[p], i[p] = cmul(r[p], i[p], twiddle[p : p + 1, :], twiddle[4 + p : 5 + p, :])
    x = split(jnp.concatenate(r + i, axis=0))
    o = mm3((table[0], table[1]), x, ((1,), (1,)))
    yr = o[:128, :128] - o[128:, 128:]
    yi = o[:128, 128:] + o[128:, :128]
    lane = lax.broadcasted_iota(jnp.int32, (1, 128), 1)
    sign = jnp.where(((lane // 32) & core) == 1, -1.0, 1.0)
    yr, yi = cmul(yr, yi, post[0] * sign, post[1] * sign)
    for c1 in range(4):
        for p in range(4):
            piece = [
                y[16 * (2 * c1 + c2) : 16 * (2 * c1 + c2) + 16, 32 * p : 32 * p + 32]
                for y in (yr, yi)
                for c2 in range(2)
            ]
            out[pl.ds(4 * p + c1, 16, stride=16), :] = jnp.concatenate(piece, axis=1)


def sums_kernel(doppler, weight, a, b, gradient, own, other):
    core = lax.axis_index("co")
    for out, half in ((own, core), (other, 1 - core)):

        def tile(j, _, out=out, half=half):
            cols = pl.ds(pl.multiple_of(half * 512 + 128 * j, 128), 128)
            here = pl.ds(pl.multiple_of(128 * j, 128), 128)
            acc = None
            for v in range(16):
                d, w = doppler[v], weight[v]
                wd = w * d
                w1 = w * (0.78125 - 0.03125 * d * d)
                ar, ai = a[0, v, :, cols], a[1, v, :, cols]
                br, bi = b[0, v, :, cols], b[1, v, :, cols]
                new = (
                    w1 * ar, w1 * ai, wd * ar, wd * ai, w * ar, w * ai,
                    w * br, w * bi, wd * br, wd * bi,
                )
                acc = new if acc is None else tuple(x + y for x, y in zip(acc, new))
            r1r, r1i, r2r, r2i, s2r, s2i, s4r, s4i, t4r, t4i = acc
            g = 0.03125 * gradient[:, cols]
            out[0, :, here] = r1r + 0.1875 * r2i
            out[1, :, here] = r1i - 0.1875 * r2r
            out[2, :, here] = s2r
            out[3, :, here] = s2i
            out[4, :, here] = 0.215625 * s4r + 0.03125 * t4i + g * s4i
            out[5, :, here] = 0.215625 * s4i - 0.03125 * t4r - g * s4r
            return 0

        lax.fori_loop(0, 4, tile, 0)


def pack_kernel(own, other, fields, out):
    for k in range(6):
        s = own[k] + other[k]
        s = jnp.concatenate([s[:, 128 * c : 128 * c + 128] for c in range(4)], axis=0).T
        for c2 in range(2):
            out[pl.ds(2 * k + c2, 64, stride=16), :] = s[64 * c2 : 64 * c2 + 64]
    for c1 in range(4):
        out[pl.ds(12 + c1, 64, stride=16), :] = fields[pl.ds(c1, 64, stride=4), :]


def columns_kernel(d0, d1, d2, d3, got, right, left, twiddle, wave, pre, out):
    def transform(xr, xi):
        yr, yi = cmul(xr, xi, pre[0], pre[1])
        y = split(jnp.concatenate([yr.T, yi.T], axis=0))
        o = mm3(y, (right[0], right[1]), ((1,), (0,)))
        ur = o[:128, :128] - o[128:, 128:]
        ui = o[:128, 128:] + o[128:, :128]
        vr, vi = cmul(ur, ui, twiddle[0], twiddle[1])
        v = split(jnp.concatenate([vr, vi], axis=1))
        o = mm3((left[0], left[1]), v, ((1,), (0,)))
        wr = o[:128, :128] - o[128:, 128:]
        wi = o[:128, 128:] + o[128:, :128]
        return cmul(wr, wi, wave[0], wave[1])

    x0, x1 = (
        jnp.concatenate([got[pl.ds(16 * f + 12 + c1, 32, stride=32), :] for c1 in range(4)], axis=0)
        for f in range(2)
    )
    low = lax.broadcasted_iota(jnp.int32, (128, 128), 1) < 64
    xr = jnp.where(low, x0, pltpu.roll(x1, 64, 1))
    xi = jnp.where(low, pltpu.roll(x0, 64, 1), x1)
    zr, zi = transform(xr, xi)
    for y in range(2):
        for f in range(2):
            for c2 in range(2):
                at = slice(64 * f + 32 * c2, 64 * f + 32 * c2 + 32)
                out[pl.ds(16 * y + 4 * f + c2, 32, stride=32), :] = zr[at]
                out[pl.ds(16 * y + 4 * f + 2 + c2, 32, stride=32), :] = zi[at]

    gr = jnp.float32(0.0)
    gi = jnp.float32(0.0)
    for d in (d0, d1, d2, d3):
        for v in range(16):
            gr = gr + d[0, v]
            gi = gi + d[0, v] * d[1, v]
    gr, gi = 0.21875 * gr, -0.03125 * gi

    def total(k):
        return jnp.concatenate(
            [
                got[pl.ds(2 * k + c2, 32, stride=32), :] + got[pl.ds(16 + 2 * k + c2, 32, stride=32), :]
                for c2 in range(2)
            ],
            axis=0,
        )

    s1r, s1i, s2r, s2i, s3r, s3i = (total(k) for k in range(6))
    er, ei, cr, ci = zr[:64], zi[:64], zr[64:], zi[64:]
    q = 0.03125 * (cr * cr + ci * ci)
    tr = s1r - q * s2r - (cr * s3i + ci * s3r) - (er * gi + ei * gr)
    ti = s1i - q * s2i + (cr * s3r - ci * s3i) + (er * gr - ei * gi)
    pr = er - 0.03125 * ti
    pi = ei + 0.03125 * tr
    zr, zi = transform(jnp.concatenate([pr, cr], axis=0), jnp.concatenate([pi, ci], axis=0))
    for y in range(2):
        for c1 in range(4):
            at = slice(32 * c1, 32 * c1 + 32)
            out[pl.ds(16 * y + 8 + c1, 32, stride=32), :] = zr[at]
            out[pl.ds(16 * y + 12 + c1, 32, stride=32), :] = zi[at]


def step_kernel(doppler, own, other, a, b, gradient, a_out, b_out, fields):
    core = lax.axis_index("co")

    @pl.when(pl.program_id(0) == 0)
    def _():
        for got, half in ((own, core), (other, 1 - core)):
            for k in range(4):
                x = jnp.concatenate([got[pl.ds(2 * k + c2, 64, stride=16), :] for c2 in range(2)], axis=0).T
                for c1 in range(4):
                    cols = pl.ds(pl.multiple_of(half * 512 + 128 * c1, 128), 128)
                    fields[k, :, cols] = x[32 * c1 : 32 * c1 + 32]

    rows = pl.ds(pl.multiple_of(8 * pl.program_id(0), 8), 8)

    def tile(j, _):
        cols = pl.ds(pl.multiple_of(128 * j, 128), 128)
        er, ei, cr, ci = (fields[k, rows, cols] for k in range(4))
        d = gradient[:, cols]
        d3 = 0.03125 * d
        q = 0.03125 * (cr * cr + ci * ci)
        wr, wi = d3 * cr - 0.215625 * ci, 0.215625 * cr + d3 * ci
        vr, vi = d3 * cr + 0.215625 * ci, 0.215625 * cr - d3 * ci
        lr = 0.9753125 - d3 * d - q
        li = -0.24375 * d
        yr = -0.03125 * (cr * er + ci * ei)
        yi = -0.03125 * (cr * ei - ci * er)
        fr, fi = -0.21875 * ei, 0.21875 * er
        for v in range(16):
            dv = doppler[v]
            dv3 = 0.03125 * dv
            kr = 0.78125 - dv3 * dv
            ki = -0.1875 * dv
            ar, ai = a[0, v, :, cols], a[1, v, :, cols]
            br, bi = b[0, v, :, cols], b[1, v, :, cols]
            mr = kr - q
            gr, gi = dv3 * cr, dv3 * ci
            ur, ui = wr + gr, wi + gi
            tr, ti = vr + gr, vi - gi
            a_out[0, v, :, cols] = (mr * ar - ki * ai) + (ur * br - ui * bi) + (fr + dv3 * er)
            a_out[1, v, :, cols] = (mr * ai + ki * ar) + (ur * bi + ui * br) + (fi + dv3 * ei)
            b_out[0, v, :, cols] = (lr * br - li * bi) + (tr * ar - ti * ai) + yr
            b_out[1, v, :, cols] = (lr * bi + li * br) + (tr * ai + ti * ar) + yi
        return 0

    lax.fori_loop(0, 8, tile, 0)


def last_kernel(own, other, pre, table, twiddle, post, probe_out, control_out):
    zero = lax.axis_index("co") == 0
    x = []
    for k in range(4):
        parts = []
        for comp in range(2):
            pieces = []
            for h in range(2):
                for c1 in range(4):
                    at = pl.ds(16 * k + 8 + 4 * comp + c1, 16, stride=64)
                    mine, theirs = own[at, :], other[at, :]
                    pieces.append(jnp.where(zero, *((mine, theirs) if h == 0 else (theirs, mine))))
            z = jnp.concatenate(pieces, axis=0).T
            z = [jnp.concatenate([z[64 * f : 64 * f + 32], z[64 * f + 32 : 64 * f + 64]], axis=1) for f in range(2)]
            parts.append(jnp.concatenate(z, axis=0))
        x.extend(cmul(*parts, pre[k : k + 1, :], pre[4 + k : 5 + k, :]))
    o = mm3(split(jnp.concatenate(x, axis=0)), (table[0], table[1]), ((1,), (0,)))
    r, i = [], []
    for k in range(4):
        top, low = o[128 * k : 128 * k + 64], o[128 * k + 64 : 128 * k + 128]
        yr = top[:, :256] - low[:, 256:]
        yi = top[:, 256:] + low[:, :256]
        if k:
            yr, yi = cmul(yr, yi, twiddle[k : k + 1, :], twiddle[4 + k : 5 + k, :])
        r.append(yr)
        i.append(yi)
    r, i = butterfly(r, i)
    for k in range(4):
        at = slice(256 * k, 256 * k + 256)
        yr, yi = cmul(r[k], i[k], post[0:1, at], post[1:2, at])
        probe_out[0, :, at], probe_out[1, :, at] = yr[:32], yi[:32]
        control_out[0, :, at], control_out[1, :, at] = yr[32:], yi[32:]


SMEM = pl.BlockSpec(memory_space=pltpu.SMEM)
VMEM = pl.BlockSpec(memory_space=pltpu.VMEM)


def whole(kernel, count, shapes, scalars=0, **kwargs):
    return pl.pallas_call(
        kernel,
        out_shape=shapes,
        in_specs=[SMEM] * scalars + [VMEM] * count,
        out_specs=jax.tree.map(lambda _: VMEM, shapes),
        **kwargs,
    )


def f32(*shape):
    return jax.ShapeDtypeStruct(shape, F32)


STATE = pl.BlockSpec((2, 16, 8, N), lambda i: (0, 0, i, 0))
SHIFT = pl.BlockSpec((8, N), lambda i: (i, 0))


def shards(probe, control, optical, spin, doppler, weight, gradient):
    swap = [(0, 1), (1, 0)]
    both = [(k, 3 - k) for k in range(4)]
    mine = jnp.stack([weight, doppler])
    shifts = (
        mine,
        lax.ppermute(mine, "co", swap),
        lax.ppermute(mine, "yh", swap),
        lax.ppermute(mine, ("yh", "co"), both),
    )
    sums = pl.BlockSpec((6, 8, 512), lambda i: (0, i, 0))
    own, other = pl.pallas_call(
        sums_kernel,
        grid=(4,),
        out_shape=(f32(6, 32, 512), f32(6, 32, 512)),
        in_specs=[SMEM, SMEM, STATE, STATE, SHIFT],
        out_specs=(sums, sums),
        name="sums",
    )(doppler, weight, optical, spin, gradient)
    other = lax.ppermute(other, "co", swap)
    tables = [jnp.asarray(t) for t in row_tables()]
    fields = whole(rows_kernel, 6, f32(256, 128), name="rows")(probe, control, *tables)
    message = whole(pack_kernel, 3, f32(N, 128), name="pack")(own, other, fields)

    def exchange(x):
        x = lax.all_to_all(x.reshape(64, 16, 128), ("space", "yh"), 0, 0, tiled=True)
        return x.reshape(N, 128)

    tables = [jnp.asarray(t) for t in column_tables()]
    message = whole(columns_kernel, 6, f32(N, 128), 4, name="columns")(
        *shifts, exchange(message), *tables
    )
    got = exchange(message)
    other = lax.ppermute(got, "co", swap)
    optical_out, spin_out = pl.pallas_call(
        step_kernel,
        grid=(4,),
        out_shape=(f32(*optical.shape), f32(*spin.shape)),
        in_specs=[SMEM, VMEM, VMEM, STATE, STATE, SHIFT],
        out_specs=(STATE, STATE),
        scratch_shapes=[pltpu.VMEM((4, 32, N), F32)],
        name="step",
    )(doppler, got, other, optical, spin, gradient)
    tables = [jnp.asarray(t) for t in last_tables()]
    probe_out, control_out = whole(last_kernel, 6, (f32(2, 32, N), f32(2, 32, N)), name="last")(
        got, other, *tables
    )
    return probe_out, control_out, optical_out, spin_out


def solution(mesh):
    fine = Mesh(mesh.devices.reshape(mesh.devices.shape[0], 2, 2), ("space", "yh", "co"))
    vel = ("yh", "co")
    field, state = P(None, "space", None), P(None, vel, "space", None)
    return jax.shard_map(
        shards,
        mesh=fine,
        in_specs=(field, field, state, state, P(vel), P(vel), P("space", None)),
        out_specs=(field, field, state, state),
        check_vma=False,
    )
```

time: 205 us -> 75.7 us (0.37); the launches traced: 202 us -> 75.3 us
  matrix products: 58.8 us -> 0 us
  other arithmetic: 30.2 us -> 0.01 us
  local copies, waits for them, and re-layouts: 30.8 us -> 2.34 us
  Pallas kernels: 0 us -> 26.8 us
  blocking collectives: 38.4 us -> 16 us
  waiting for transfers between devices: 18.7 us -> 10.1 us
  starting transfers between devices: 23.2 us -> 19.3 us
    dot_general x17 -> x0, matrix products: 58.8 us -> none  [the longest x8 33.4 us: product_of(): return jnp.einsum('mn,fnk->fmk', table, values, precision=HIGHEST)]
    pallas_call x0 -> x6, Pallas kernels: none -> 26.8 us  [the longest x1 9.43 us: shards(): pl.pallas_call(step_kernel, grid=(4,), out_shape=(f32(*optical.shape), f3...]
    all_to_all x3 -> x1, blocking collectives: 38.4 us -> 16 us  [exchange(): lax.all_to_all(x.reshape(64, 16, 128), ('space', 'yh'), 0, 0, tiled=True)]
    unnamed x48 -> x20, local copies, waits for them, and re-layouts: 18.7 us -> 2.34 us
    sub x5 -> x0, other arithmetic: 15.1 us -> none  [the longest x2 11.7 us: derivative(): -DEPHASE * spin_real + gradient * spin_imag]
    all_to_all x4 -> x1, waiting for transfers between devices: 18.7 us -> 4.91 us  [exchange(): lax.all_to_all(x.reshape(64, 16, 128), ('space', 'yh'), 0, 0, tiled=True)]
    all_to_all x4 -> x1, starting transfers between devices: 23.2 us -> 11.2 us  [exchange(): lax.all_to_all(x.reshape(64, 16, 128), ('space', 'yh'), 0, 0, tiled=True)]
    add x3 -> x0, other arithmetic: 10.4 us -> none  [the longest x2 7.52 us: midpoint(): return (optical + DT * rate_optical, spin_part + DT * rate_spin)]
  transfers between devices with their start and end apart: 4 -> 6, of which waited for: 4 -> 4; matrix products, arithmetic and copies ran while one was open for 7% -> 0% of each run, Pallas kernels for 0% -> 3%
where the time goes in v1:
time: 75.7 us; the launch traced here: 75.3 us
  Pallas kernels  26.8 us (35%)
  starting transfers between devices  19.3 us (25%)
  blocking collectives  16 us (21%)
  waiting for transfers between devices  10.1 us (13%)
  local copies, waits for them, and re-layouts  2.34 us (3%)
    all_to_all x1, blocking collectives, exchange(): lax.all_to_all(x.reshape(64, 16, 128), ('space', 'yh'), 0, 0, tiled=True)  16 us
    all_to_all x1, starting transfers between devices, exchange(): lax.all_to_all(x.reshape(64, 16, 128), ('space', 'yh'), 0, 0, tiled=True)  11.2 us
    pallas_call x1, Pallas kernels, shards(): pl.pallas_call(step_kernel, grid=(4,), out_shape=(f32(*optical.shape), f3...  9.43 us
    pallas_call x1, Pallas kernels, shards(): pl.pallas_call(sums_kernel, grid=(4,), out_shape=(f32(6, 32, 512), f32(6,...  5.81 us
    all_to_all x1, waiting for transfers between devices, exchange(): lax.all_to_all(x.reshape(64, 16, 128), ('space', 'yh'), 0, 0, tiled=True)  4.91 us
    pallas_call x1, Pallas kernels, shards(): whole(columns_kernel, 6, f32(N, 128), 4, name='columns')  4.04 us
    ppermute x1, starting transfers between devices, shards(): lax.ppermute(mine, ('yh', 'co'), both)  3.04 us
    pallas_call x1, Pallas kernels, shards(): whole(last_kernel, 6, (f32(2, 32, N), f32(2, 32, N)), name='last')  3.04 us
  transfers between devices with their start and end apart: 6, of which 4 were waited for; matrix products, arithmetic and copies ran while one was open for 0% of the time, Pallas kernels for 3%

profile of v1, /device:TPU:1, one launch (start us, length us, event | category | flops | bytes accessed | tf_op | source)
XLA Modules:
  0.0 75.3 jit_solution(5915085502726829900)
XLA Ops:
  0.6 0.0 copy-start.4
  0.6 0.0 copy-start.6
  0.7 5.8 %sums.1 = (f32[6,32,512]{2,1,0:T(8,128)}, f32[6,32,512]{2,1,0:T(8,128)}) custom-call(f32[16]{0:T(128)} %doppler.3, f32[16]{0:T(128)} %weight.1, f32[2,16,32,1024]{3,2,1,0:T(8,128)} %a.3, f32[2,16,32,1024]{3,2,1,0:T(8,128)} %b.3, f32[32,1024]{1,0:T(8,128)} %gradient.3), custom_call_target="tpu_custom_call" | custom-call | tf_op jit(solution)/shard_map/sums/pallas_call | solution.py:347
  6.5 1.4 %collective-permute-start.3 = (f32[6,32,512]{2,1,0:T(8,128)}, f32[6,32,512]{2,1,0:T(8,128)S(1)}, u32[]{:S(2)}, u32[]{:S(2)}) collective-permute-start(f32[6,32,512]{2,1,0:T(8,128)} %get-tuple-element.11), channel_id=1, source_target_pairs={{0,1},{1,0},{2,3},{3,2},{4,5},{5,4},{6,7},{7,6},{8,9},{9,8},{10,11... | collective-permute-start | bytes 1179656 | tf_op jit(solution)/shard_map/ppermute | solution.py:355
  7.8 2.3 %rows.1.fields = f32[256,128]{1,0:T(8,128)} custom-call(f32[2,32,1024]{2,1,0:T(8,128)} %probe.1, f32[2,32,1024]{2,1,0:T(8,128)} %control.1, f32[2,1024]{1,0:T(2,128)} %constant.24.clone.pre, f32[8,256]{1,0:T(8,128)} %constant.25.clone.twiddle, bf16[2,256,256]{2,1,0:T(8,128)(2,1)} %constant.26.clone.table, f32[2,128,128]{2,1,0:T(8,128)} %constant.27.clone.post), custom_call_target="tpu_custom_call" | custom-call | tf_op jit(solution)/shard_map/rows/pallas_call | solution.py:357
  10.2 0.0 collective-permute-done.3.other
  10.2 0.0 copy-start.3
  10.2 0.7 copy-done.3
  10.9 2.2 %pack.1 = f32[1024,128]{1,0:T(8,128)} custom-call(f32[6,32,512]{2,1,0:T(8,128)} %get-tuple-element.10.own, f32[6,32,512]{2,1,0:T(8,128)} %copy-done.3, f32[256,128]{1,0:T(8,128)} %rows.1.fields), custom_call_target="tpu_custom_call" | custom-call | tf_op jit(solution)/shard_map/pack/pallas_call | solution.py:358
  13.1 11.2 %all-to-all-start = ((f32[64,16,128]{2,1,0:T(8,128)}), f32[64,16,128]{2,1,0:T(8,128)S(1)}, u32[]{:S(2)}, u32[]{:S(2)}) async-start(f32[64,16,128]{2,1,0:T(8,128)} %bitcast.11), calls=%async_computation | async-start | bytes 1048576 | tf_op jit(solution)/shard_map/all_to_all | solution.py:361
  24.4 0.0 copy-done.4
  24.4 0.0 copy-done.6
  24.4 0.0 copy-start.5
  24.4 3.0 %collective-permute-start.2 = (f32[2,16]{1,0:T(2,128)S(1)}, f32[2,16]{1,0:T(2,128)S(1)}, u32[]{:S(2)}, u32[]{:S(2)}) collective-permute-start(f32[2,16]{1,0:T(2,128)S(1)} %pad_maximum_fusion.d0), channel_id=1, source_target_pairs={{0,3},{1,2},{2,1},{3,0},{4,7},{5,6},{6,5},{7,4},{8,11},{9,10},{10,... | collective-permute-start | bytes 392 | tf_op jit(solution)/shard_map/ppermute | solution.py:344
  27.5 0.2 collective-permute-start.1
  27.6 0.5 collective-permute-start
  28.1 1.5 %collective-permute-done.2.d3 = f32[2,16]{1,0:T(2,128)S(1)} collective-permute-done((f32[2,16]{1,0:T(2,128)S(1)}, f32[2,16]{1,0:T(2,128)S(1)}, u32[]{:S(2)}, u32[]{:S(2)}) %collective-permute-start.2) | collective-permute-done | bytes 160 | tf_op jit(solution)/shard_map/ppermute | solution.py:344
  29.7 0.0 copy-start.7
  29.7 2.1 %collective-permute-done.1.d2 = f32[2,16]{1,0:T(2,128)S(1)} collective-permute-done((f32[2,16]{1,0:T(2,128)S(1)}, f32[2,16]{1,0:T(2,128)S(1)}, u32[]{:S(2)}, u32[]{:S(2)}) %collective-permute-start.1) | collective-permute-done | bytes 160 | tf_op jit(solution)/shard_map/ppermute | solution.py:343
  31.8 0.0 copy-start.8
  31.8 0.0 collective-permute-done.d1
  31.8 0.0 copy-start.9
  31.8 4.9 %all-to-all-done = f32[64,16,128]{2,1,0:T(8,128)S(1)} async-done(((f32[64,16,128]{2,1,0:T(8,128)}), f32[64,16,128]{2,1,0:T(8,128)S(1)}, u32[]{:S(2)}, u32[]{:S(2)}) %all-to-all-start) | async-done | bytes 524320 | tf_op jit(solution)/shard_map/all_to_all | solution.py:361
  36.7 0.0 copy-start.2
  36.7 0.0 copy-done.5
  36.7 0.0 copy-done.7
  36.7 0.0 copy-done.8
  36.7 0.0 copy-done.9
  36.7 0.8 %copy-done.2 = f32[64,16,128]{2,1,0:T(8,128)} copy-done((f32[64,16,128]{2,1,0:T(8,128)}, f32[64,16,128]{2,1,0:T(8,128)S(1)}, u32[]{:S(2)}) %copy-start.2) | copy-done | bytes 524312
  37.5 4.0 %columns.1 = f32[1024,128]{1,0:T(8,128)} custom-call(f32[2,16]{1,0:T(2,128)} %copy-done.5, f32[2,16]{1,0:T(2,128)} %copy-done.9, f32[2,16]{1,0:T(2,128)} %copy-done.8, f32[2,16]{1,0:T(2,128)} %copy-done.7, f32[1024,128]{1,0:T(8,128)} %bitcast.9, bf16[2,128,256]{2,1,0:T(8,128)(2,1)} %constant.28.clone.right, bf16[2,256,128]{2,1,0:T(8,128)(2,1)} %constant.29.clone.left, ...), custom_call_target="tpu_custom_call" | custom-call | tf_op jit(solution)/shard_map/columns/pallas_call | solution.py:365
  41.5 16.0 %all_to_all.10 = f32[64,16,128]{2,1,0:T(8,128)S(1)} all-to-all(f32[64,16,128]{2,1,0:T(8,128)} %bitcast.10), channel_id=1, replica_groups=mesh['space'=32,'yh'=2,'co'=2] {'space','yh'}, dimensions={0} | all-to-all | bytes 1048576 | tf_op jit(solution)/shard_map/all_to_all | solution.py:361
  57.5 0.0 copy-start
  57.5 3.0 %collective-permute-start.4 = (f32[1024,128]{1,0:T(8,128)S(1)}, f32[1024,128]{1,0:T(8,128)S(1)}, u32[]{:S(2)}, u32[]{:S(2)}) collective-permute-start(f32[1024,128]{1,0:T(8,128)S(1)} %bitcast.6), channel_id=1, source_target_pairs={{0,1},{1,0},{2,3},{3,2},{4,5},{5,4},{6,7},{7,6},{8,9},{9,8},{10,11... | collective-permute-start | bytes 1572872 | tf_op jit(solution)/shard_map/ppermute | solution.py:369
  60.5 1.5 %collective-permute-done.4.other = f32[1024,128]{1,0:T(8,128)S(1)} collective-permute-done((f32[1024,128]{1,0:T(8,128)S(1)}, f32[1024,128]{1,0:T(8,128)S(1)}, u32[]{:S(2)}, u32[]{:S(2)}) %collective-permute-start.4) | collective-permute-done | bytes 524320 | tf_op jit(solution)/shard_map/ppermute | solution.py:369
  62.0 0.0 copy-done
  62.0 0.0 copy-start.1
  62.0 0.8 %copy-done.1 = f32[1024,128]{1,0:T(8,128)} copy-done((f32[1024,128]{1,0:T(8,128)}, f32[1024,128]{1,0:T(8,128)S(1)}, u32[]{:S(2)}) %copy-start.1) | copy-done | bytes 524312
  62.8 9.4 %step.1 = (f32[2,16,32,1024]{3,2,1,0:T(8,128)}, f32[2,16,32,1024]{3,2,1,0:T(8,128)}) custom-call(f32[16]{0:T(128)} %doppler.3, f32[1024,128]{1,0:T(8,128)} %bitcast.7, f32[1024,128]{1,0:T(8,128)} %copy-done.1, f32[2,16,32,1024]{3,2,1,0:T(8,128)} %a.3, f32[2,16,32,1024]{3,2,1,0:T(8,128)} %b.3, f32[32,1024]{1,0:T(8,128)} %gradient.3), custom_call_target="tpu_custom_call" | custom-call | tf_op jit(solution)/shard_map/step/pallas_call | solution.py:370
  72.2 3.0 %last.1 = (f32[2,32,1024]{2,1,0:T(8,128)}, f32[2,32,1024]{2,1,0:T(8,128)}) custom-call(f32[1024,128]{1,0:T(8,128)} %bitcast.8, f32[1024,128]{1,0:T(8,128)} %copy-done.1, f32[8,256]{1,0:T(8,128)} %constant.33.clone.pre, bf16[2,256,512]{2,1,0:T(8,128)(2,1)} %constant.34.clone.table, f32[8,256]{1,0:T(8,128)} %constant.25.clone.twiddle, ...), custom_call_target="tpu_custom_call" | custom-call | tf_op jit(solution)/shard_map/last/pallas_call | solution.py:380
  (1 shorter events, 0.0 us)
Async XLA Ops:
  0.6 23.7 %copy-start.4 = (f32[16]{0:T(128)S(1)}, f32[16]{0:T(128)}, u32[]{:S(2)}) copy-start(f32[16]{0:T(128)} %doppler.3) | copy-start | bytes 196
  0.6 23.7 %copy-start.6 = (f32[16]{0:T(128)S(1)}, f32[16]{0:T(128)}, u32[]{:S(2)}) copy-start(f32[16]{0:T(128)} %weight.1) | copy-start | bytes 196
  6.5 3.7 %collective-permute-start.3 = (f32[6,32,512]{2,1,0:T(8,128)}, f32[6,32,512]{2,1,0:T(8,128)S(1)}, u32[]{:S(2)}, u32[]{:S(2)}) collective-permute-start(f32[6,32,512]{2,1,0:T(8,128)} %get-tuple-element.11), channel_id=1, source_target_pairs={{0,1},{1,0},{2,3},{3,2},{4,5},{5,4},{6,7},{7,6},{8,9},{9,8},{10,11... | collective-permute-start | bytes 1179656 | tf_op jit(solution)/shard_map/ppermute | solution.py:355
  10.2 0.7 copy-start.3
  13.1 23.6 %all-to-all-start = ((f32[64,16,128]{2,1,0:T(8,128)}), f32[64,16,128]{2,1,0:T(8,128)S(1)}, u32[]{:S(2)}, u32[]{:S(2)}) async-start(f32[64,16,128]{2,1,0:T(8,128)} %bitcast.11), calls=%async_computation | async-start | bytes 1048576 | tf_op jit(solution)/shard_map/all_to_all | solution.py:361
  24.4 12.3 %copy-start.5 = (f32[2,16]{1,0:T(2,128)}, f32[2,16]{1,0:T(2,128)S(1)}, u32[]{:S(2)}) copy-start(f32[2,16]{1,0:T(2,128)S(1)} %pad_maximum_fusion.d0) | copy-start | bytes 388
  24.4 5.3 %collective-permute-start.2 = (f32[2,16]{1,0:T(2,128)S(1)}, f32[2,16]{1,0:T(2,128)S(1)}, u32[]{:S(2)}, u32[]{:S(2)}) collective-permute-start(f32[2,16]{1,0:T(2,128)S(1)} %pad_maximum_fusion.d0), channel_id=1, source_target_pairs={{0,3},{1,2},{2,1},{3,0},{4,7},{5,6},{6,5},{7,4},{8,11},{9,10},{10,... | collective-permute-start | bytes 392 | tf_op jit(solution)/shard_map/ppermute | solution.py:344
  27.5 4.3 %collective-permute-start.1 = (f32[2,16]{1,0:T(2,128)S(1)}, f32[2,16]{1,0:T(2,128)S(1)}, u32[]{:S(2)}, u32[]{:S(2)}) collective-permute-start(f32[2,16]{1,0:T(2,128)S(1)} %pad_maximum_fusion.d0), channel_id=1, source_target_pairs={{0,2},{2,0},{1,3},{3,1},{4,6},{6,4},{5,7},{7,5},{8,10},{10,8},{9,1... | collective-permute-start | bytes 392 | tf_op jit(solution)/shard_map/ppermute | solution.py:343
  27.6 4.1 %collective-permute-start = (f32[2,16]{1,0:T(2,128)S(1)}, f32[2,16]{1,0:T(2,128)S(1)}, u32[]{:S(2)}, u32[]{:S(2)}) collective-permute-start(f32[2,16]{1,0:T(2,128)S(1)} %pad_maximum_fusion.d0), channel_id=1, source_target_pairs={{0,1},{1,0},{2,3},{3,2},{4,5},{5,4},{6,7},{7,6},{8,9},{9,8},{10,11... | collective-permute-start | bytes 392 | tf_op jit(solution)/shard_map/ppermute | solution.py:342
  29.7 7.0 %copy-start.7 = (f32[2,16]{1,0:T(2,128)}, f32[2,16]{1,0:T(2,128)S(1)}, u32[]{:S(2)}) copy-start(f32[2,16]{1,0:T(2,128)S(1)} %collective-permute-done.2.d3) | copy-start | bytes 388
  31.8 4.9 %copy-start.8 = (f32[2,16]{1,0:T(2,128)}, f32[2,16]{1,0:T(2,128)S(1)}, u32[]{:S(2)}) copy-start(f32[2,16]{1,0:T(2,128)S(1)} %collective-permute-done.1.d2) | copy-start | bytes 388
  31.8 4.9 %copy-start.9 = (f32[2,16]{1,0:T(2,128)}, f32[2,16]{1,0:T(2,128)S(1)}, u32[]{:S(2)}) copy-start(f32[2,16]{1,0:T(2,128)S(1)} %collective-permute-done.d1) | copy-start | bytes 388
  36.7 0.8 %copy-start.2 = (f32[64,16,128]{2,1,0:T(8,128)}, f32[64,16,128]{2,1,0:T(8,128)S(1)}, u32[]{:S(2)}) copy-start(f32[64,16,128]{2,1,0:T(8,128)S(1)} %all-to-all-done) | copy-start | bytes 1572868
  57.5 4.5 %copy-start = (f32[64,16,128]{2,1,0:T(8,128)}, f32[64,16,128]{2,1,0:T(8,128)S(1)}, u32[]{:S(2)}) copy-start(f32[64,16,128]{2,1,0:T(8,128)S(1)} %all_to_all.10) | copy-start | bytes 1572868
  57.5 4.5 %collective-permute-start.4 = (f32[1024,128]{1,0:T(8,128)S(1)}, f32[1024,128]{1,0:T(8,128)S(1)}, u32[]{:S(2)}, u32[]{:S(2)}) collective-permute-start(f32[1024,128]{1,0:T(8,128)S(1)} %bitcast.6), channel_id=1, source_target_pairs={{0,1},{1,0},{2,3},{3,2},{4,5},{5,4},{6,7},{7,6},{8,9},{9,8},{10,11... | collective-permute-start | bytes 1572872 | tf_op jit(solution)/shard_map/ppermute | solution.py:369
  62.0 0.8 %copy-start.1 = (f32[1024,128]{1,0:T(8,128)}, f32[1024,128]{1,0:T(8,128)S(1)}, u32[]{:S(2)}) copy-start(f32[1024,128]{1,0:T(8,128)S(1)} %collective-permute-done.4.other) | copy-start | bytes 1572868

commit v2 on v1

--- a/solution.py
+++ b/solution.py
@@ -96,14 +96,10 @@
     )
 
 
-def rows_kernel(probe, control, pre, twiddle, table, post, out):
-    core, half = lax.axis_index("co"), lax.axis_index("yh")
-    first = half == 0
-    xr = jnp.where(first, probe[0], control[0])
-    xi = jnp.where(first, probe[1], control[1])
+def rows_part(x, core, pre, twiddle, table, post, out):
     lane = lax.broadcasted_iota(jnp.int32, (1, N), 1)
     sign = jnp.where((lane & core) == 1, -1.0, 1.0)
-    xr, xi = cmul(xr, xi, pre[0:1, :] * sign, pre[1:2, :] * sign)
+    xr, xi = cmul(x[0], x[1], pre[0:1, :] * sign, pre[1:2, :] * sign)
     r, i = butterfly(
         [xr[:, 256 * k : 256 * k + 256] for k in range(4)],
         [xi[:, 256 * k : 256 * k + 256] for k in range(4)],
@@ -127,33 +123,100 @@
             out[pl.ds(4 * p + c1, 16, stride=16), :] = jnp.concatenate(piece, axis=1)
 
 
-def sums_kernel(doppler, weight, a, b, gradient, own, other):
-    core = lax.axis_index("co")
-    for out, half in ((own, core), (other, 1 - core)):
-
-        def tile(j, _, out=out, half=half):
-            cols = pl.ds(pl.multiple_of(half * 512 + 128 * j, 128), 128)
+def front_kernel(
+    doppler_hbm, weight_hbm, a_hbm, b_hbm, probe, control, gradient_hbm, pre_hbm, twiddle_hbm, table_hbm, post_hbm,
+    own, other, fields, a, b, gradient, rates, x, pre, twiddle, table, post, doppler, weight, state_sem, sem,
+):
+    core, half = lax.axis_index("co"), lax.axis_index("yh")
+    small = [
+        pltpu.make_async_copy(src, dst, sem.at[k])
+        for k, (src, dst) in enumerate(
+            (
+                (pre_hbm, pre),
+                (twiddle_hbm, twiddle),
+                (table_hbm, table),
+                (post_hbm, post),
+                (gradient_hbm, gradient),
+                (doppler_hbm, doppler),
+                (weight_hbm, weight),
+            )
+        )
+    ]
+
+    @pl.when(half == 0)
+    def _():
+        pltpu.make_async_copy(probe, x, sem.at[7]).start()
+
+    @pl.when(half == 1)
+    def _():
+        pltpu.make_async_copy(control, x, sem.at[7]).start()
+
+    for copy in small:
+        copy.start()
+
+    def chunk(n):
+        rows = pl.ds(8 * (n // 2), 8)
+        cols = pl.ds(pl.multiple_of((core if n % 2 else 1 - core) * 512, 512), 512)
+        return [
+            pltpu.make_async_copy(src.at[:, :, rows, cols], dst.at[:, :, rows, cols], state_sem.at[m, n])
+            for m, (src, dst) in enumerate(((a_hbm, a), (b_hbm, b)))
+        ]
+
+    def start(n):
+        for copy in chunk(n):
+            copy.start()
+
+    ahead = 4
+    for n in range(ahead):
+        start(n)
+
+    pltpu.make_async_copy(probe, x, sem.at[7]).wait()
+    for copy in small:
+        copy.wait()
+    rows_part(x, core, pre, twiddle, table, post, fields)
+    gr, gi = 0.0, 0.0
+    for v in range(16):
+        gr = gr + weight[v]
+        gi = gi + weight[v] * doppler[v]
+    first = lax.broadcasted_iota(jnp.int32, (8, 512), 0) == 0
+    for out in (own, other):
+        out[192:200, :] = jnp.where(first, 0.21875 * gr, -0.03125 * gi)
+    for v in range(16):
+        d = doppler[v]
+        for m, c in enumerate((0.03125 * d, 0.78125 - 0.03125 * d * d, -0.1875 * d)):
+            rates[3 * v + m] = jnp.full((8, 128), c, F32)
+
+    for n in range(8):
+        for copy in chunk(n):
+            copy.wait()
+        if n + ahead < 8:
+            start(n + ahead)
+        k = n // 2
+        rows = pl.ds(8 * k, 8)
+        out, part = (own, core) if n % 2 else (other, 1 - core)
+
+        def tile(j, _, out=out, part=part, rows=rows, k=k):
+            cols = pl.ds(pl.multiple_of(part * 512 + 128 * j, 128), 128)
             here = pl.ds(pl.multiple_of(128 * j, 128), 128)
             acc = None
             for v in range(16):
                 d, w = doppler[v], weight[v]
                 wd = w * d
                 w1 = w * (0.78125 - 0.03125 * d * d)
-                ar, ai = a[0, v, :, cols], a[1, v, :, cols]
-                br, bi = b[0, v, :, cols], b[1, v, :, cols]
+                ar, ai = a[0, v, rows, cols], a[1, v, rows, cols]
+                br, bi = b[0, v, rows, cols], b[1, v, rows, cols]
                 new = (
                     w1 * ar, w1 * ai, wd * ar, wd * ai, w * ar, w * ai,
                     w * br, w * bi, wd * br, wd * bi,
                 )
                 acc = new if acc is None else tuple(x + y for x, y in zip(acc, new))
             r1r, r1i, r2r, r2i, s2r, s2i, s4r, s4i, t4r, t4i = acc
-            g = 0.03125 * gradient[:, cols]
-            out[0, :, here] = r1r + 0.1875 * r2i
-            out[1, :, here] = r1i - 0.1875 * r2r
-            out[2, :, here] = s2r
-            out[3, :, here] = s2i
-            out[4, :, here] = 0.215625 * s4r + 0.03125 * t4i + g * s4i
-            out[5, :, here] = 0.215625 * s4i - 0.03125 * t4r - g * s4r
+            g = 0.03125 * gradient[rows, cols]
+            s3r = 0.215625 * s4r + 0.03125 * t4i + g * s4i
+            s3i = 0.215625 * s4i - 0.03125 * t4r - g * s4r
+            s1r, s1i = r1r + 0.1875 * r2i, r1i - 0.1875 * r2r
+            for m, s in enumerate((s1r, s1i, s2r, s2i, s3r, s3i)):
+                out[pl.ds(32 * m + 8 * k, 8), here] = s
             return 0
 
         lax.fori_loop(0, 4, tile, 0)
@@ -161,15 +224,18 @@
 
 def pack_kernel(own, other, fields, out):
     for k in range(6):
-        s = own[k] + other[k]
+        s = own[32 * k : 32 * k + 32, :] + other[32 * k : 32 * k + 32, :]
         s = jnp.concatenate([s[:, 128 * c : 128 * c + 128] for c in range(4)], axis=0).T
         for c2 in range(2):
-            out[pl.ds(2 * k + c2, 64, stride=16), :] = s[64 * c2 : 64 * c2 + 64]
+            out[pl.ds(2 * k + c2, 64, stride=17), :] = s[64 * c2 : 64 * c2 + 64]
     for c1 in range(4):
-        out[pl.ds(12 + c1, 64, stride=16), :] = fields[pl.ds(c1, 64, stride=4), :]
-
-
-def columns_kernel(d0, d1, d2, d3, got, right, left, twiddle, wave, pre, out):
+        out[pl.ds(12 + c1, 64, stride=17), :] = fields[pl.ds(c1, 64, stride=4), :]
+    real = lax.broadcasted_iota(jnp.int32, (1, 128), 1) < 64
+    g = own[192:194, :128] + other[192:194, :128]
+    out[pl.ds(16, 64, stride=17), :] = jnp.broadcast_to(jnp.where(real, g[0:1], g[1:2]), (64, 128))
+
+
+def columns_kernel(got, right, left, twiddle, wave, pre, out):
     def transform(xr, xi):
         yr, yi = cmul(xr, xi, pre[0], pre[1])
         y = split(jnp.concatenate([yr.T, yi.T], axis=0))
@@ -184,7 +250,7 @@
         return cmul(wr, wi, wave[0], wave[1])
 
     x0, x1 = (
-        jnp.concatenate([got[pl.ds(16 * f + 12 + c1, 32, stride=32), :] for c1 in range(4)], axis=0)
+        jnp.concatenate([got[pl.ds(17 * f + 12 + c1, 32, stride=34), :] for c1 in range(4)], axis=0)
         for f in range(2)
     )
     low = lax.broadcasted_iota(jnp.int32, (128, 128), 1) < 64
@@ -198,18 +264,13 @@
                 out[pl.ds(16 * y + 4 * f + c2, 32, stride=32), :] = zr[at]
                 out[pl.ds(16 * y + 4 * f + 2 + c2, 32, stride=32), :] = zi[at]
 
-    gr = jnp.float32(0.0)
-    gi = jnp.float32(0.0)
-    for d in (d0, d1, d2, d3):
-        for v in range(16):
-            gr = gr + d[0, v]
-            gi = gi + d[0, v] * d[1, v]
-    gr, gi = 0.21875 * gr, -0.03125 * gi
+    g = got[16:17, :] + got[33:34, :]
+    gr, gi = g[:, 0:1], g[:, 64:65]
 
     def total(k):
         return jnp.concatenate(
             [
-                got[pl.ds(2 * k + c2, 32, stride=32), :] + got[pl.ds(16 + 2 * k + c2, 32, stride=32), :]
+                got[pl.ds(2 * k + c2, 32, stride=34), :] + got[pl.ds(17 + 2 * k + c2, 32, stride=34), :]
                 for c2 in range(2)
             ],
             axis=0,
@@ -230,54 +291,56 @@
             out[pl.ds(16 * y + 12 + c1, 32, stride=32), :] = zi[at]
 
 
-def step_kernel(doppler, own, other, a, b, gradient, a_out, b_out, fields):
-    core = lax.axis_index("co")
-
-    @pl.when(pl.program_id(0) == 0)
-    def _():
-        for got, half in ((own, core), (other, 1 - core)):
-            for k in range(4):
-                x = jnp.concatenate([got[pl.ds(2 * k + c2, 64, stride=16), :] for c2 in range(2)], axis=0).T
-                for c1 in range(4):
-                    cols = pl.ds(pl.multiple_of(half * 512 + 128 * c1, 128), 128)
-                    fields[k, :, cols] = x[32 * c1 : 32 * c1 + 32]
-
-    rows = pl.ds(pl.multiple_of(8 * pl.program_id(0), 8), 8)
-
-    def tile(j, _):
-        cols = pl.ds(pl.multiple_of(128 * j, 128), 128)
-        er, ei, cr, ci = (fields[k, rows, cols] for k in range(4))
-        d = gradient[:, cols]
-        d3 = 0.03125 * d
-        q = 0.03125 * (cr * cr + ci * ci)
-        wr, wi = d3 * cr - 0.215625 * ci, 0.215625 * cr + d3 * ci
-        vr, vi = d3 * cr + 0.215625 * ci, 0.215625 * cr - d3 * ci
-        lr = 0.9753125 - d3 * d - q
-        li = -0.24375 * d
-        yr = -0.03125 * (cr * er + ci * ei)
-        yi = -0.03125 * (cr * ei - ci * er)
-        fr, fi = -0.21875 * ei, 0.21875 * er
-        for v in range(16):
-            dv = doppler[v]
-            dv3 = 0.03125 * dv
-            kr = 0.78125 - dv3 * dv
-            ki = -0.1875 * dv
-            ar, ai = a[0, v, :, cols], a[1, v, :, cols]
-            br, bi = b[0, v, :, cols], b[1, v, :, cols]
-            mr = kr - q
-            gr, gi = dv3 * cr, dv3 * ci
-            ur, ui = wr + gr, wi + gi
-            tr, ti = vr + gr, vi - gi
-            a_out[0, v, :, cols] = (mr * ar - ki * ai) + (ur * br - ui * bi) + (fr + dv3 * er)
-            a_out[1, v, :, cols] = (mr * ai + ki * ar) + (ur * bi + ui * br) + (fi + dv3 * ei)
-            b_out[0, v, :, cols] = (lr * br - li * bi) + (tr * ar - ti * ai) + yr
-            b_out[1, v, :, cols] = (lr * bi + li * br) + (tr * ai + ti * ar) + yi
-        return 0
-
-    lax.fori_loop(0, 8, tile, 0)
-
-
-def last_kernel(own, other, pre, table, twiddle, post, probe_out, control_out):
+def place(got, fields):
+    for k in range(4):
+        x = jnp.concatenate([got[pl.ds(2 * k + c2, 64, stride=16), :] for c2 in range(2)], axis=0).T
+        for c1 in range(4):
+            fields[k, :, 128 * c1 : 128 * c1 + 128] = x[32 * c1 : 32 * c1 + 32]
+
+
+def half_step(part, rates, fields, a, b, gradient, a_out, b_out, a_buf, b_buf, sem):
+    copies = []
+    for k in range(4):
+        rows = pl.ds(8 * k, 8)
+
+        def tile(j, _, rows=rows):
+            cols = pl.ds(pl.multiple_of(part * 512 + 128 * j, 128), 128)
+            here = pl.ds(pl.multiple_of(128 * j, 128), 128)
+            er, ei, cr, ci = (fields[m, rows, here] for m in range(4))
+            d = gradient[rows, cols]
+            d3 = 0.03125 * d
+            q = 0.03125 * (cr * cr + ci * ci)
+            wr, wi = d3 * cr - 0.215625 * ci, 0.215625 * cr + d3 * ci
+            vr, vi = d3 * cr + 0.215625 * ci, 0.215625 * cr - d3 * ci
+            lr = 0.9753125 - d3 * d - q
+            li = -0.24375 * d
+            yr = -0.03125 * (cr * er + ci * ei)
+            yi = -0.03125 * (cr * ei - ci * er)
+            fr, fi = -0.21875 * ei, 0.21875 * er
+            for v in range(16):
+                dv3, kr, ki = (rates[3 * v + m] for m in range(3))
+                ar, ai = a[0, v, rows, cols], a[1, v, rows, cols]
+                br, bi = b[0, v, rows, cols], b[1, v, rows, cols]
+                mr = kr - q
+                gr, gi = dv3 * cr, dv3 * ci
+                ur, ui = wr + gr, wi + gi
+                tr, ti = vr + gr, vi - gi
+                a_buf[0, v, rows, here] = (mr * ar - ki * ai) + (ur * br - ui * bi) + (fr + dv3 * er)
+                a_buf[1, v, rows, here] = (mr * ai + ki * ar) + (ur * bi + ui * br) + (fi + dv3 * ei)
+                b_buf[0, v, rows, here] = (lr * br - li * bi) + (tr * ar - ti * ai) + yr
+                b_buf[1, v, rows, here] = (lr * bi + li * br) + (tr * ai + ti * ar) + yi
+            return 0
+
+        lax.fori_loop(0, 4, tile, 0)
+        cols = pl.ds(pl.multiple_of(part * 512, 128), 512)
+        for n, (src, dst) in enumerate(((a_buf, a_out), (b_buf, b_out))):
+            copy = pltpu.make_async_copy(src.at[:, :, rows, :], dst.at[:, :, rows, cols], sem.at[n, k])
+            copy.start()
+            copies.append(copy)
+    return copies
+
+
+def last_part(own, other, pre, table, twiddle, post, probe_out, control_out):
     zero = lax.axis_index("co") == 0
     x = []
     for k in range(4):
@@ -311,76 +374,126 @@
         control_out[0, :, at], control_out[1, :, at] = yr[32:], yi[32:]
 
 
-SMEM = pl.BlockSpec(memory_space=pltpu.SMEM)
+def near_kernel(rates, got, a, b, gradient, a_out, b_out, fields, a_buf, b_buf, sem):
+    place(got, fields)
+    part = lax.axis_index("co")
+    for copy in half_step(part, rates, fields, a, b, gradient, a_out, b_out, a_buf, b_buf, sem):
+        copy.wait()
+
+
+def far_kernel(
+    rates, own, other, a, b, gradient, pre, table, twiddle, post, a_in, b_in,
+    a_out, b_out, probe_out, control_out, fields, a_buf, b_buf, sem,
+):
+    del a_in, b_in
+    place(other, fields)
+    part = 1 - lax.axis_index("co")
+    copies = half_step(part, rates, fields, a, b, gradient, a_out, b_out, a_buf, b_buf, sem)
+    last_part(own, other, pre, table, twiddle, post, probe_out, control_out)
+    for copy in copies:
+        copy.wait()
+
+
 VMEM = pl.BlockSpec(memory_space=pltpu.VMEM)
 
 
-def whole(kernel, count, shapes, scalars=0, **kwargs):
-    return pl.pallas_call(
-        kernel,
-        out_shape=shapes,
-        in_specs=[SMEM] * scalars + [VMEM] * count,
-        out_specs=jax.tree.map(lambda _: VMEM, shapes),
-        **kwargs,
-    )
+ANY = pl.BlockSpec(memory_space=pl.ANY)
 
 
 def f32(*shape):
     return jax.ShapeDtypeStruct(shape, F32)
 
 
-STATE = pl.BlockSpec((2, 16, 8, N), lambda i: (0, 0, i, 0))
-SHIFT = pl.BlockSpec((8, N), lambda i: (i, 0))
+def near(*shape):
+    return pltpu.VMEM(shape, F32)
+
+
+def pinned(arrays):
+    return [pltpu.with_memory_space_constraint(jnp.asarray(x), pltpu.VMEM) for x in arrays]
+
+
+def far(arrays):
+    return [pltpu.with_memory_space_constraint(jnp.asarray(x), pltpu.HBM) for x in arrays]
+
+
+def limit(mib):
+    return pltpu.CompilerParams(vmem_limit_bytes=mib << 20)
 
 
 def shards(probe, control, optical, spin, doppler, weight, gradient):
     swap = [(0, 1), (1, 0)]
-    both = [(k, 3 - k) for k in range(4)]
-    mine = jnp.stack([weight, doppler])
-    shifts = (
-        mine,
-        lax.ppermute(mine, "co", swap),
-        lax.ppermute(mine, "yh", swap),
-        lax.ppermute(mine, ("yh", "co"), both),
-    )
-    sums = pl.BlockSpec((6, 8, 512), lambda i: (0, i, 0))
-    own, other = pl.pallas_call(
-        sums_kernel,
-        grid=(4,),
-        out_shape=(f32(6, 32, 512), f32(6, 32, 512)),
-        in_specs=[SMEM, SMEM, STATE, STATE, SHIFT],
-        out_specs=(sums, sums),
-        name="sums",
-    )(doppler, weight, optical, spin, gradient)
+    tables = [jnp.asarray(t) for t in row_tables()]
+    dma = pltpu.SemaphoreType.DMA
+    state = optical.shape
+    own, other, fields, optical, spin, gradient, rates = pl.pallas_call(
+        front_kernel,
+        out_shape=(near(200, 512), near(200, 512), near(256, 128), near(*state), near(*state), near(32, N), near(48, 8, 128)),
+        in_specs=[ANY] * 11,
+        out_specs=(VMEM,) * 7,
+        scratch_shapes=[
+            pltpu.VMEM((2, 32, N), F32),
+            *(pltpu.VMEM(t.shape, t.dtype) for t in tables),
+            pltpu.SMEM((16,), F32),
+            pltpu.SMEM((16,), F32),
+            dma((2, 8)),
+            dma((8,)),
+        ],
+        compiler_params=limit(6),
+        name="front",
+    )(*far([doppler, weight, optical, spin, probe, control, gradient, *tables]))
     other = lax.ppermute(other, "co", swap)
-    tables = [jnp.asarray(t) for t in row_tables()]
-    fields = whole(rows_kernel, 6, f32(256, 128), name="rows")(probe, control, *tables)
-    message = whole(pack_kernel, 3, f32(N, 128), name="pack")(own, other, fields)
+    message = pl.pallas_call(
+        pack_kernel,
+        out_shape=near(17 * 64, 128),
+        in_specs=[VMEM] * 3,
+        out_specs=VMEM,
+        compiler_params=limit(6),
+        name="pack",
+    )(*pinned([own, other, fields]))
 
     def exchange(x):
-        x = lax.all_to_all(x.reshape(64, 16, 128), ("space", "yh"), 0, 0, tiled=True)
-        return x.reshape(N, 128)
-
-    tables = [jnp.asarray(t) for t in column_tables()]
-    message = whole(columns_kernel, 6, f32(N, 128), 4, name="columns")(
-        *shifts, exchange(message), *tables
-    )
+        shape = x.shape
+        x = lax.all_to_all(x.reshape(64, -1, 1, 128), ("space", "yh"), 0, 0, tiled=True)
+        return x.reshape(shape)
+
+    tables = column_tables()
+    message = pl.pallas_call(
+        columns_kernel,
+        out_shape=near(N, 128),
+        in_specs=[VMEM] * (1 + len(tables)),
+        out_specs=VMEM,
+        compiler_params=limit(6),
+        name="columns",
+    )(*pinned([exchange(message), *tables]))
     got = exchange(message)
     other = lax.ppermute(got, "co", swap)
-    optical_out, spin_out = pl.pallas_call(
-        step_kernel,
-        grid=(4,),
-        out_shape=(f32(*optical.shape), f32(*spin.shape)),
-        in_specs=[SMEM, VMEM, VMEM, STATE, STATE, SHIFT],
-        out_specs=(STATE, STATE),
-        scratch_shapes=[pltpu.VMEM((4, 32, N), F32)],
-        name="step",
-    )(doppler, got, other, optical, spin, gradient)
-    tables = [jnp.asarray(t) for t in last_tables()]
-    probe_out, control_out = whole(last_kernel, 6, (f32(2, 32, N), f32(2, 32, N)), name="last")(
-        got, other, *tables
-    )
-    return probe_out, control_out, optical_out, spin_out
+    scratch = [
+        pltpu.VMEM((4, 32, 512), F32),
+        pltpu.VMEM((2, 16, 32, 512), F32),
+        pltpu.VMEM((2, 16, 32, 512), F32),
+        dma((2, 4)),
+    ]
+    halfway = pl.pallas_call(
+        near_kernel,
+        out_shape=(f32(*state), f32(*state)),
+        in_specs=[VMEM] * 5,
+        out_specs=(ANY, ANY),
+        scratch_shapes=scratch,
+        compiler_params=limit(8),
+        name="near",
+    )(*pinned([rates, got, optical, spin, gradient]))
+    tables = last_tables()
+    optical, spin, probe, control = pl.pallas_call(
+        far_kernel,
+        out_shape=(f32(*state), f32(*state), f32(2, 32, N), f32(2, 32, N)),
+        in_specs=[VMEM] * (6 + len(tables)) + [ANY] * 2,
+        out_specs=(ANY, ANY, VMEM, VMEM),
+        scratch_shapes=scratch,
+        input_output_aliases={10: 0, 11: 1},
+        compiler_params=limit(12),
+        name="far",
+    )(*pinned([rates, got, other, optical, spin, gradient, *tables]), *halfway)
+    return probe, control, optical, spin
 
 
 def solution(mesh):

time: 75.7 us -> 59.9 us (0.79)
  blocking collectives: 16 us -> 38.8 us
  starting transfers between devices: 19.3 us -> 4.82 us
  Pallas kernels: 26.8 us -> 13.9 us
  waiting for transfers between devices: 10.1 us -> 1.38 us
  local copies, waits for them, and re-layouts: 2.34 us -> 0.05 us
    all_to_all x1 -> x2, blocking collectives: 16 us -> 38.8 us  [exchange(): lax.all_to_all(x.reshape(64, -1, 1, 128), ('space', 'yh'), 0, 0, tiled=True)]
    pallas_call x6 -> x5, Pallas kernels: 26.8 us -> 13.9 us  [the longest x1 5.37 us: shards(): pl.pallas_call(front_kernel, out_shape=(near(200, 512), near(200, 512), n...]
    all_to_all x1 -> x0, starting transfers between devices: 11.2 us -> none  [exchange(): lax.all_to_all(x.reshape(64, 16, 128), ('space', 'yh'), 0, 0, tiled=True)]
    all_to_all x1 -> x0, waiting for transfers between devices: 4.91 us -> none  [exchange(): lax.all_to_all(x.reshape(64, 16, 128), ('space', 'yh'), 0, 0, tiled=True)]
    ppermute x3 -> x0, starting transfers between devices: 3.72 us -> none  [the longest x1 3.04 us: shards(): lax.ppermute(mine, ('yh', 'co'), both)]
    ppermute x3 -> x0, waiting for transfers between devices: 3.62 us -> none  [the longest x1 2.07 us: shards(): lax.ppermute(mine, 'yh', swap)]
    unnamed x20 -> x18, local copies, waits for them, and re-layouts: 2.34 us -> 0.05 us
    ppermute x1, waiting for transfers between devices: 1.54 us -> 0.01 us  [shards(): other = lax.ppermute(got, 'co', swap)]
  transfers between devices with their start and end apart: 6 -> 2, of which waited for: 4 -> 1; matrix products, arithmetic and copies ran while one was open for 0% -> 0% of each run, Pallas kernels for 3% -> 5%
where the time goes in v2:
time: 59.9 us; the launch traced here: 59.7 us
  blocking collectives  38.8 us (65%)
  Pallas kernels  13.9 us (23%)
  starting transfers between devices  4.82 us (8%)
  waiting for transfers between devices  1.38 us (2%)
  between operations  0.77 us (1%)
    all_to_all x2, blocking collectives, exchange(): lax.all_to_all(x.reshape(64, -1, 1, 128), ('space', 'yh'), 0, 0, tiled=True)  38.8 us
    pallas_call x1, Pallas kernels, shards(): pl.pallas_call(front_kernel, out_shape=(near(200, 512), near(200, 512), n...  5.37 us
    pallas_call x1, Pallas kernels, shards(): pl.pallas_call(far_kernel, out_shape=(f32(*state), f32(*state), f32(2, 32...  3.81 us
    ppermute x1, starting transfers between devices, shards(): other = lax.ppermute(got, 'co', swap)  3.36 us
    pallas_call x1, Pallas kernels, shards(): pl.pallas_call(near_kernel, out_shape=(f32(*state), f32(*state)), in_spec...  2.79 us
    pallas_call x1, Pallas kernels, shards(): pl.pallas_call(columns_kernel, out_shape=near(N, 128), in_specs=[VMEM] *...  1.78 us
    ppermute x1, starting transfers between devices, shards(): other = lax.ppermute(other, 'co', swap)  1.46 us
    ppermute x1, waiting for transfers between devices, shards(): other = lax.ppermute(other, 'co', swap)  1.37 us
  transfers between devices with their start and end apart: 2, of which 1 were waited for; matrix products, arithmetic and copies ran while one was open for 0% of the time, Pallas kernels for 5%

profile of v2, /device:TPU:1, one launch (start us, length us, event | category | flops | bytes accessed | tf_op | source)
XLA Modules:
  0.0 59.7 jit_solution(8404825471885214915)
XLA Ops:
  0.6 0.0 copy-start.1
  0.6 0.0 copy-start.2
  0.7 0.0 copy-start.3
  0.7 0.0 copy-start.4
  0.7 0.0 copy-start.5
  0.7 5.4 %front.1 = (f32[200,512]{1,0:T(8,128)S(1)}, f32[200,512]{1,0:T(8,128)S(1)}, f32[256,128]{1,0:T(8,128)S(1)}, f32[2,16,32,1024]{3,2,1,0:T(8,128)S(1)}, f32[2,16,32...) custom-call(f32[16]{0:T(128)} %doppler_hbm.1, f32[16]{0:T(128)} %weight_hbm.1, ...), custom_call_target="tpu_custom_call" | custom-call | tf_op jit(solution)/shard_map/front/pallas_call | solution.py:428
  6.1 1.5 %collective-permute-start = (f32[200,512]{1,0:T(8,128)S(1)}, f32[200,512]{1,0:T(8,128)S(1)}, u32[]{:S(2)}, u32[]{:S(2)}) collective-permute-start(f32[200,512]{1,0:T(8,128)S(1)} %get-tuple-element.19), channel_id=1, source_target_pairs={{0,1},{1,0},{2,3},{3,2},{4,5},{5,4},{6,7},{7,6},{8,9},{9,8},{10,11... | collective-permute-start | bytes 1228808 | tf_op jit(solution)/shard_map/ppermute | solution.py:444
  7.5 1.4 %collective-permute-done.other = f32[200,512]{1,0:T(8,128)S(1)} collective-permute-done((f32[200,512]{1,0:T(8,128)S(1)}, f32[200,512]{1,0:T(8,128)S(1)}, u32[]{:S(2)}, u32[]{:S(2)}) %collective-permute-start) | collective-permute-done | bytes 409632 | tf_op jit(solution)/shard_map/ppermute | solution.py:444
  8.9 0.2 pack.1
  9.1 23.5 %all_to_all.10 = f32[64,17,1,128]{3,2,1,0:T(1,128)S(1)} all-to-all(f32[64,17,1,128]{3,2,1,0:T(1,128)S(1)} %bitcast.9), channel_id=1, replica_groups=mesh['space'=32,'yh'=2,'co'=2] {'space','yh'}, dimensions={0} | all-to-all | bytes 1114112 | tf_op jit(solution)/shard_map/all_to_all | solution.py:456
  32.6 0.0 copy-done.1
  32.6 0.0 copy-done.2
  32.6 0.0 copy-done.3
  32.6 0.0 copy-done.4
  32.6 0.0 copy-done.5
  32.6 1.8 %columns.1 = f32[1024,128]{1,0:T(8,128)S(1)} custom-call(f32[1088,128]{1,0:T(8,128)S(1)} %bitcast.10, bf16[2,128,256]{2,1,0:T(8,128)(2,1)S(1)} %copy-done.5, bf16[2,256,128]{2,1,0:T(8,128)(2,1)S(1)} %copy-done.4, f32[2,128,128]{2,1,0:T(8,128)S(1)} %copy-done.3, f32[2,128,128]{2,1,0:T(8,128)S(1)} %copy-done.2, f32[2,128,128]{2,1,0:T(8,128)S(1)} %copy-done.1), custom_call_target="tpu_custom_call" | custom-call | tf_op jit(solution)/shard_map/columns/pallas_call | solution.py:460
  34.4 15.3 %all_to_all.11 = f32[64,16,1,128]{3,1,2,0:T(8,128)S(1)} all-to-all(f32[64,16,1,128]{3,1,2,0:T(8,128)S(1)} %bitcast.11), channel_id=1, replica_groups=mesh['space'=32,'yh'=2,'co'=2] {'space','yh'}, dimensions={0} | all-to-all | bytes 1048576 | tf_op jit(solution)/shard_map/all_to_all | solution.py:456
  49.7 3.4 %collective-permute-start.1 = (f32[1024,128]{1,0:T(8,128)S(1)}, f32[1024,128]{1,0:T(8,128)S(1)}, u32[]{:S(2)}, u32[]{:S(2)}) collective-permute-start(f32[1024,128]{1,0:T(8,128)S(1)} %bitcast.6), channel_id=1, source_target_pairs={{0,1},{1,0},{2,3},{3,2},{4,5},{5,4},{6,7},{7,6},{8,9},{9,8},{10,11... | collective-permute-start | bytes 1572872 | tf_op jit(solution)/shard_map/ppermute | solution.py:469
  53.1 0.0 copy-start
  53.1 0.0 copy-start.6
  53.1 0.0 copy-start.7
  53.1 0.0 copy-start.8
  53.1 2.8 %near.1 = (f32[2,16,32,1024]{3,2,1,0:T(8,128)}, f32[2,16,32,1024]{3,2,1,0:T(8,128)}) custom-call(f32[48,8,128]{2,1,0:T(8,128)S(1)} %get-tuple-element.17.rates, f32[1024,128]{1,0:T(8,128)S(1)} %bitcast.7, f32[2,16,32,1024]{3,2,1,0:T(8,128)S(1)} %get-tuple-element.21.a, f32[2,16,32,1024]{3,2,1,0:T(8,128)S(1)} %get-tuple-element.22.b, ...), custom_call_target="tpu_custom_call" | custom-call | tf_op jit(solution)/shard_map/near/pallas_call | solution.py:476
  55.9 0.0 collective-permute-done.1.other
  55.9 0.0 copy-done
  55.9 0.0 copy-done.6
  55.9 0.0 copy-done.7
  55.9 0.0 copy-done.8
  55.9 3.8 %far.1 = (f32[2,16,32,1024]{3,2,1,0:T(8,128)}, f32[2,16,32,1024]{3,2,1,0:T(8,128)}, f32[2,32,1024]{2,1,0:T(8,128)}, f32[2,32,1024]{2,1,0:T(8,128)}) custom-call(f32[48,8,128]{2,1,0:T(8,128)S(1)} %get-tuple-element.17.rates, f32[1024,128]{1,0:T(8,128)S(1)} %bitcast.8, ...), custom_call_target="tpu_custom_call", output_to_operand_aliasing={{0}: (10, {}), {1}: (11, {})} | custom-call | tf_op jit(solution)/shard_map/far/pallas_call | solution.py:486
Async XLA Ops:
  0.6 31.9 %copy-start.1 = (f32[2,128,128]{2,1,0:T(8,128)S(1)}, f32[2,128,128]{2,1,0:T(8,128)}, u32[]{:S(2)}) copy-start(f32[2,128,128]{2,1,0:T(8,128)} %constant.32.clone.pre) | copy-start | bytes 393220
  0.6 31.9 %copy-start.2 = (f32[2,128,128]{2,1,0:T(8,128)S(1)}, f32[2,128,128]{2,1,0:T(8,128)}, u32[]{:S(2)}) copy-start(f32[2,128,128]{2,1,0:T(8,128)} %constant.31.clone.wave) | copy-start | bytes 393220
  0.7 31.9 %copy-start.3 = (f32[2,128,128]{2,1,0:T(8,128)S(1)}, f32[2,128,128]{2,1,0:T(8,128)}, u32[]{:S(2)}) copy-start(f32[2,128,128]{2,1,0:T(8,128)} %constant.30.clone.twiddle) | copy-start | bytes 393220
  0.7 31.9 %copy-start.4 = (bf16[2,256,128]{2,1,0:T(8,128)(2,1)S(1)}, bf16[2,256,128]{2,1,0:T(8,128)(2,1)}, u32[]{:S(2)}) copy-start(bf16[2,256,128]{2,1,0:T(8,128)(2,1)} %constant.29.clone.left) | copy-start | bytes 393220
  0.7 31.9 %copy-start.5 = (bf16[2,128,256]{2,1,0:T(8,128)(2,1)S(1)}, bf16[2,128,256]{2,1,0:T(8,128)(2,1)}, u32[]{:S(2)}) copy-start(bf16[2,128,256]{2,1,0:T(8,128)(2,1)} %constant.28.clone.right) | copy-start | bytes 393220
  6.1 2.8 %collective-permute-start = (f32[200,512]{1,0:T(8,128)S(1)}, f32[200,512]{1,0:T(8,128)S(1)}, u32[]{:S(2)}, u32[]{:S(2)}) collective-permute-start(f32[200,512]{1,0:T(8,128)S(1)} %get-tuple-element.19), channel_id=1, source_target_pairs={{0,1},{1,0},{2,3},{3,2},{4,5},{5,4},{6,7},{7,6},{8,9},{9,8},{10,11... | collective-permute-start | bytes 1228808 | tf_op jit(solution)/shard_map/ppermute | solution.py:444
  49.7 6.2 %collective-permute-start.1 = (f32[1024,128]{1,0:T(8,128)S(1)}, f32[1024,128]{1,0:T(8,128)S(1)}, u32[]{:S(2)}, u32[]{:S(2)}) collective-permute-start(f32[1024,128]{1,0:T(8,128)S(1)} %bitcast.6), channel_id=1, source_target_pairs={{0,1},{1,0},{2,3},{3,2},{4,5},{5,4},{6,7},{7,6},{8,9},{9,8},{10,11... | collective-permute-start | bytes 1572872 | tf_op jit(solution)/shard_map/ppermute | solution.py:469
  53.1 2.8 %copy-start = (bf16[2,256,512]{2,1,0:T(8,128)(2,1)S(1)}, bf16[2,256,512]{2,1,0:T(8,128)(2,1)}, u32[]{:S(2)}) copy-start(bf16[2,256,512]{2,1,0:T(8,128)(2,1)} %constant.34.clone.table) | copy-start | bytes 1572868
  53.1 2.8 %copy-start.6 = (f32[8,256]{1,0:T(8,128)S(1)}, f32[8,256]{1,0:T(8,128)}, u32[]{:S(2)}) copy-start(f32[8,256]{1,0:T(8,128)} %constant.25.clone.twiddle_hbm.twiddle) | copy-start | bytes 24580
  53.1 2.8 %copy-start.7 = (f32[2,1024]{1,0:T(2,128)S(1)}, f32[2,1024]{1,0:T(2,128)}, u32[]{:S(2)}) copy-start(f32[2,1024]{1,0:T(2,128)} %constant.35.clone.post) | copy-start | bytes 24580
  53.1 2.8 %copy-start.8 = (f32[8,256]{1,0:T(8,128)S(1)}, f32[8,256]{1,0:T(8,128)}, u32[]{:S(2)}) copy-start(f32[8,256]{1,0:T(8,128)} %constant.33.clone.pre) | copy-start | bytes 24580

commit v3 on v2

--- a/solution.py
+++ b/solution.py
@@ -50,11 +50,11 @@
 def column_tables():
     eye = np.eye(4)
     small = turn(-np.arange(32)[:, None] * np.arange(32)[None, :], 32)
-    right = np.concatenate([np.kron(eye, small.real), np.kron(eye, small.imag)], axis=1)
-    inner = np.tile(np.arange(32), 4)
-    twiddle = pair(turn(-inner[:, None] * inner[None, :], N))
-    wave = chirp(32 * inner[:, None] + inner[None, :])
-    return halves(right), halves(right.T), twiddle, pair(wave), pair(NORM * wave)
+    norm = NORM * small
+    right = np.concatenate([np.kron(eye, norm.real), np.kron(eye, norm.imag)], axis=1)
+    left = np.concatenate([np.kron(eye, small.real), np.kron(eye, small.imag)], axis=0)
+    outer, inner = np.arange(32)[:, None], np.tile(np.arange(32), 4)[None, :]
+    return halves(right), halves(left), pair(turn(-outer * inner, N)), pair(chirp(32 * outer + inner))
 
 
 def last_tables():
@@ -235,9 +235,11 @@
     out[pl.ds(16, 64, stride=17), :] = jnp.broadcast_to(jnp.where(real, g[0:1], g[1:2]), (64, 128))
 
 
-def columns_kernel(got, right, left, twiddle, wave, pre, out):
+def columns_kernel(got, right, left, twiddle, wave, out):
+    twiddle, wave = ([jnp.concatenate([t[k]] * 4, axis=0) for k in range(2)] for t in (twiddle, wave))
+
     def transform(xr, xi):
-        yr, yi = cmul(xr, xi, pre[0], pre[1])
+        yr, yi = cmul(xr, xi, wave[0], wave[1])
         y = split(jnp.concatenate([yr.T, yi.T], axis=0))
         o = mm3(y, (right[0], right[1]), ((1,), (0,)))
         ur = o[:128, :128] - o[128:, 128:]
@@ -383,13 +385,16 @@
 
 def far_kernel(
     rates, own, other, a, b, gradient, pre, table, twiddle, post, a_in, b_in,
-    a_out, b_out, probe_out, control_out, fields, a_buf, b_buf, sem,
+    a_out, b_out, probe_out, control_out, fields, a_buf, b_buf, sem, probe_buf, control_buf, last_sem,
 ):
     del a_in, b_in
     place(other, fields)
     part = 1 - lax.axis_index("co")
     copies = half_step(part, rates, fields, a, b, gradient, a_out, b_out, a_buf, b_buf, sem)
-    last_part(own, other, pre, table, twiddle, post, probe_out, control_out)
+    last_part(own, other, pre, table, twiddle, post, probe_buf, control_buf)
+    for k, (src, dst) in enumerate(((probe_buf, probe_out), (control_buf, control_out))):
+        copies.append(pltpu.make_async_copy(src, dst, last_sem.at[k]))
+        copies[-1].start()
     for copy in copies:
         copy.wait()
 
@@ -487,8 +492,8 @@
         far_kernel,
         out_shape=(f32(*state), f32(*state), f32(2, 32, N), f32(2, 32, N)),
         in_specs=[VMEM] * (6 + len(tables)) + [ANY] * 2,
-        out_specs=(ANY, ANY, VMEM, VMEM),
-        scratch_shapes=scratch,
+        out_specs=(ANY,) * 4,
+        scratch_shapes=scratch + [pltpu.VMEM((2, 32, N), F32), pltpu.VMEM((2, 32, N), F32), dma((2,))],
         input_output_aliases={10: 0, 11: 1},
         compiler_params=limit(12),
         name="far",

time: 59.9 us -> 59.6 us (level)
  no operation moved by 1% of the time
where the time goes in v3:
time: 59.6 us; the launch traced here: 59.4 us
  blocking collectives  38.8 us (65%)
  Pallas kernels  13.6 us (23%)
  starting transfers between devices  4.82 us (8%)
  waiting for transfers between devices  1.38 us (2%)
  between operations  0.76 us (1%)
    all_to_all x2, blocking collectives, exchange(): lax.all_to_all(x.reshape(64, -1, 1, 128), ('space', 'yh'), 0, 0, tiled=True)  38.8 us
    pallas_call x1, Pallas kernels, shards(): pl.pallas_call(front_kernel, out_shape=(near(200, 512), near(200, 512), n...  5.36 us
    pallas_call x1, Pallas kernels, shards(): pl.pallas_call(far_kernel, out_shape=(f32(*state), f32(*state), f32(2, 32...  3.53 us
    ppermute x1, starting transfers between devices, shards(): other = lax.ppermute(got, 'co', swap)  3.36 us
    pallas_call x1, Pallas kernels, shards(): pl.pallas_call(near_kernel, out_shape=(f32(*state), f32(*state)), in_spec...  2.79 us
    pallas_call x1, Pallas kernels, shards(): pl.pallas_call(columns_kernel, out_shape=near(N, 128), in_specs=[VMEM] *...  1.78 us
    ppermute x1, starting transfers between devices, shards(): other = lax.ppermute(other, 'co', swap)  1.46 us
    ppermute x1, waiting for transfers between devices, shards(): other = lax.ppermute(other, 'co', swap)  1.37 us
  transfers between devices with their start and end apart: 2, of which 1 were waited for; matrix products, arithmetic and copies ran while one was open for 0% of the time, Pallas kernels for 5%

profile of v3, /device:TPU:1, one launch (start us, length us, event | category | flops | bytes accessed | tf_op | source)
XLA Modules:
  0.0 59.4 jit_solution(12338610785211883949)
XLA Ops:
  0.6 0.0 copy-start.1
  0.6 0.0 copy-start.2
  0.7 0.0 copy-start.4
  0.7 0.0 copy-start.5
  0.7 5.4 %front.1 = (f32[200,512]{1,0:T(8,128)S(1)}, f32[200,512]{1,0:T(8,128)S(1)}, f32[256,128]{1,0:T(8,128)S(1)}, f32[2,16,32,1024]{3,2,1,0:T(8,128)S(1)}, f32[2,16,32...) custom-call(f32[16]{0:T(128)} %doppler_hbm.1, f32[16]{0:T(128)} %weight_hbm.1, ...), custom_call_target="tpu_custom_call" | custom-call | tf_op jit(solution)/shard_map/front/pallas_call | solution.py:433
  6.1 1.5 %collective-permute-start = (f32[200,512]{1,0:T(8,128)S(1)}, f32[200,512]{1,0:T(8,128)S(1)}, u32[]{:S(2)}, u32[]{:S(2)}) collective-permute-start(f32[200,512]{1,0:T(8,128)S(1)} %get-tuple-element.19), channel_id=1, source_target_pairs={{0,1},{1,0},{2,3},{3,2},{4,5},{5,4},{6,7},{7,6},{8,9},{9,8},{10,11... | collective-permute-start | bytes 1228808 | tf_op jit(solution)/shard_map/ppermute | solution.py:449
  7.5 1.4 %collective-permute-done.other = f32[200,512]{1,0:T(8,128)S(1)} collective-permute-done((f32[200,512]{1,0:T(8,128)S(1)}, f32[200,512]{1,0:T(8,128)S(1)}, u32[]{:S(2)}, u32[]{:S(2)}) %collective-permute-start) | collective-permute-done | bytes 409632 | tf_op jit(solution)/shard_map/ppermute | solution.py:449
  8.9 0.2 pack.1
  9.1 23.5 %all_to_all.10 = f32[64,17,1,128]{3,2,1,0:T(1,128)S(1)} all-to-all(f32[64,17,1,128]{3,2,1,0:T(1,128)S(1)} %bitcast.10), channel_id=1, replica_groups=mesh['space'=32,'yh'=2,'co'=2] {'space','yh'}, dimensions={0} | all-to-all | bytes 1114112 | tf_op jit(solution)/shard_map/all_to_all | solution.py:461
  32.5 0.0 copy-done.1
  32.5 0.0 copy-done.2
  32.5 0.0 copy-done.4
  32.6 0.0 copy-done.5
  32.6 1.8 %columns.1 = f32[1024,128]{1,0:T(8,128)S(1)} custom-call(f32[1088,128]{1,0:T(8,128)S(1)} %bitcast.9, bf16[2,128,256]{2,1,0:T(8,128)(2,1)S(1)} %copy-done.2, bf16[2,256,128]{2,1,0:T(8,128)(2,1)S(1)} %copy-done.1, f32[2,32,128]{2,1,0:T(8,128)S(1)} %copy-done.5, f32[2,32,128]{2,1,0:T(8,128)S(1)} %copy-done.4), custom_call_target="tpu_custom_call" | custom-call | tf_op jit(solution)/shard_map/columns/pallas_call | solution.py:465
  34.4 15.3 %all_to_all.11 = f32[64,16,1,128]{3,1,2,0:T(8,128)S(1)} all-to-all(f32[64,16,1,128]{3,1,2,0:T(8,128)S(1)} %bitcast.11), channel_id=1, replica_groups=mesh['space'=32,'yh'=2,'co'=2] {'space','yh'}, dimensions={0} | all-to-all | bytes 1048576 | tf_op jit(solution)/shard_map/all_to_all | solution.py:461
  49.7 3.4 %collective-permute-start.1 = (f32[1024,128]{1,0:T(8,128)S(1)}, f32[1024,128]{1,0:T(8,128)S(1)}, u32[]{:S(2)}, u32[]{:S(2)}) collective-permute-start(f32[1024,128]{1,0:T(8,128)S(1)} %bitcast.6), channel_id=1, source_target_pairs={{0,1},{1,0},{2,3},{3,2},{4,5},{5,4},{6,7},{7,6},{8,9},{9,8},{10,11... | collective-permute-start | bytes 1572872 | tf_op jit(solution)/shard_map/ppermute | solution.py:474
  53.0 0.0 copy-start
  53.0 0.0 copy-start.3
  53.0 0.0 copy-start.6
  53.0 0.0 copy-start.7
  53.0 2.8 %near.1 = (f32[2,16,32,1024]{3,2,1,0:T(8,128)}, f32[2,16,32,1024]{3,2,1,0:T(8,128)}) custom-call(f32[48,8,128]{2,1,0:T(8,128)S(1)} %get-tuple-element.17.rates, f32[1024,128]{1,0:T(8,128)S(1)} %bitcast.7, f32[2,16,32,1024]{3,2,1,0:T(8,128)S(1)} %get-tuple-element.21.a, f32[2,16,32,1024]{3,2,1,0:T(8,128)S(1)} %get-tuple-element.22.b, ...), custom_call_target="tpu_custom_call" | custom-call | tf_op jit(solution)/shard_map/near/pallas_call | solution.py:481
  55.9 0.0 collective-permute-done.1.other
  55.9 0.0 copy-done
  55.9 0.0 copy-done.3
  55.9 0.0 copy-done.6
  55.9 0.0 copy-done.7
  55.9 3.5 %far.1 = (f32[2,16,32,1024]{3,2,1,0:T(8,128)}, f32[2,16,32,1024]{3,2,1,0:T(8,128)}, f32[2,32,1024]{2,1,0:T(8,128)}, f32[2,32,1024]{2,1,0:T(8,128)}) custom-call(f32[48,8,128]{2,1,0:T(8,128)S(1)} %get-tuple-element.17.rates, f32[1024,128]{1,0:T(8,128)S(1)} %bitcast.8, ...), custom_call_target="tpu_custom_call", output_to_operand_aliasing={{0}: (10, {}), {1}: (11, {})} | custom-call | tf_op jit(solution)/shard_map/far/pallas_call | solution.py:491
Async XLA Ops:
  0.6 31.9 %copy-start.1 = (bf16[2,256,128]{2,1,0:T(8,128)(2,1)S(1)}, bf16[2,256,128]{2,1,0:T(8,128)(2,1)}, u32[]{:S(2)}) copy-start(bf16[2,256,128]{2,1,0:T(8,128)(2,1)} %constant.27.clone.left) | copy-start | bytes 393220
  0.6 31.9 %copy-start.2 = (bf16[2,128,256]{2,1,0:T(8,128)(2,1)S(1)}, bf16[2,128,256]{2,1,0:T(8,128)(2,1)}, u32[]{:S(2)}) copy-start(bf16[2,128,256]{2,1,0:T(8,128)(2,1)} %constant.26.clone.right) | copy-start | bytes 393220
  0.7 31.9 %copy-start.4 = (f32[2,32,128]{2,1,0:T(8,128)S(1)}, f32[2,32,128]{2,1,0:T(8,128)}, u32[]{:S(2)}) copy-start(f32[2,32,128]{2,1,0:T(8,128)} %constant.29.clone.wave) | copy-start | bytes 98308
  0.7 31.9 %copy-start.5 = (f32[2,32,128]{2,1,0:T(8,128)S(1)}, f32[2,32,128]{2,1,0:T(8,128)}, u32[]{:S(2)}) copy-start(f32[2,32,128]{2,1,0:T(8,128)} %constant.28.clone.twiddle) | copy-start | bytes 98308
  6.1 2.8 %collective-permute-start = (f32[200,512]{1,0:T(8,128)S(1)}, f32[200,512]{1,0:T(8,128)S(1)}, u32[]{:S(2)}, u32[]{:S(2)}) collective-permute-start(f32[200,512]{1,0:T(8,128)S(1)} %get-tuple-element.19), channel_id=1, source_target_pairs={{0,1},{1,0},{2,3},{3,2},{4,5},{5,4},{6,7},{7,6},{8,9},{9,8},{10,11... | collective-permute-start | bytes 1228808 | tf_op jit(solution)/shard_map/ppermute | solution.py:449
  49.7 6.2 %collective-permute-start.1 = (f32[1024,128]{1,0:T(8,128)S(1)}, f32[1024,128]{1,0:T(8,128)S(1)}, u32[]{:S(2)}, u32[]{:S(2)}) collective-permute-start(f32[1024,128]{1,0:T(8,128)S(1)} %bitcast.6), channel_id=1, source_target_pairs={{0,1},{1,0},{2,3},{3,2},{4,5},{5,4},{6,7},{7,6},{8,9},{9,8},{10,11... | collective-permute-start | bytes 1572872 | tf_op jit(solution)/shard_map/ppermute | solution.py:474
  53.0 2.8 %copy-start = (bf16[2,256,512]{2,1,0:T(8,128)(2,1)S(1)}, bf16[2,256,512]{2,1,0:T(8,128)(2,1)}, u32[]{:S(2)}) copy-start(bf16[2,256,512]{2,1,0:T(8,128)(2,1)} %constant.31.clone.table) | copy-start | bytes 1572868
  53.0 2.8 %copy-start.3 = (f32[8,256]{1,0:T(8,128)S(1)}, f32[8,256]{1,0:T(8,128)}, u32[]{:S(2)}) copy-start(f32[8,256]{1,0:T(8,128)} %constant.23.clone.twiddle_hbm.twiddle) | copy-start | bytes 24580
  53.0 2.8 %copy-start.6 = (f32[2,1024]{1,0:T(2,128)S(1)}, f32[2,1024]{1,0:T(2,128)}, u32[]{:S(2)}) copy-start(f32[2,1024]{1,0:T(2,128)} %constant.32.clone.post) | copy-start | bytes 24580
  53.0 2.8 %copy-start.7 = (f32[8,256]{1,0:T(8,128)S(1)}, f32[8,256]{1,0:T(8,128)}, u32[]{:S(2)}) copy-start(f32[8,256]{1,0:T(8,128)} %constant.30.clone.pre) | copy-start | bytes 24580

commit v4 on v3

--- a/solution.py
+++ b/solution.py
@@ -51,8 +51,10 @@
     eye = np.eye(4)
     small = turn(-np.arange(32)[:, None] * np.arange(32)[None, :], 32)
     norm = NORM * small
-    right = np.concatenate([np.kron(eye, norm.real), np.kron(eye, norm.imag)], axis=1)
-    left = np.concatenate([np.kron(eye, small.real), np.kron(eye, small.imag)], axis=0)
+    right, turned = (np.concatenate([np.kron(eye, f.real), np.kron(eye, f.imag)], axis=1) for f in (norm, 1j * norm))
+    right = np.concatenate([right, turned], axis=0)
+    left, turned = (np.concatenate([np.kron(eye, f.real), np.kron(eye, f.imag)], axis=0) for f in (small, 1j * small))
+    left = np.concatenate([left, turned], axis=1)
     outer, inner = np.arange(32)[:, None], np.tile(np.arange(32), 4)[None, :]
     return halves(right), halves(left), pair(turn(-outer * inner, N)), pair(chirp(32 * outer + inner))
 
@@ -240,15 +242,13 @@
 
     def transform(xr, xi):
         yr, yi = cmul(xr, xi, wave[0], wave[1])
-        y = split(jnp.concatenate([yr.T, yi.T], axis=0))
+        y = split(jnp.concatenate([yr.T, yi.T], axis=1))
         o = mm3(y, (right[0], right[1]), ((1,), (0,)))
-        ur = o[:128, :128] - o[128:, 128:]
-        ui = o[:128, 128:] + o[128:, :128]
-        vr, vi = cmul(ur, ui, twiddle[0], twiddle[1])
-        v = split(jnp.concatenate([vr, vi], axis=1))
-        o = mm3((left[0], left[1]), v, ((1,), (0,)))
-        wr = o[:128, :128] - o[128:, 128:]
-        wi = o[:128, 128:] + o[128:, :128]
+        vr, vi = cmul(o[:, :128], o[:, 128:], twiddle[0], twiddle[1])
+        high, low = split(jnp.concatenate([vr, vi], axis=0))
+        o = mm(left[0], jnp.concatenate([high, low], axis=1), ((1,), (0,)))
+        o = o[:, :128] + (o[:, 128:] + mm(left[1], high, ((1,), (0,))))
+        wr, wi = o[:128], o[128:]
         return cmul(wr, wi, wave[0], wave[1])
 
     x0, x1 = (

time: 59.6 us -> 59.2 us (level)
  no operation moved by 1% of the time
where the time goes in v4:
time: 59.2 us; the launch traced here: 59 us
  blocking collectives  38.8 us (66%)
  Pallas kernels  13.2 us (22%)
  starting transfers between devices  4.82 us (8%)
  waiting for transfers between devices  1.38 us (2%)
  between operations  0.76 us (1%)
    all_to_all x2, blocking collectives, exchange(): lax.all_to_all(x.reshape(64, -1, 1, 128), ('space', 'yh'), 0, 0, tiled=True)  38.8 us
    pallas_call x1, Pallas kernels, shards(): pl.pallas_call(front_kernel, out_shape=(near(200, 512), near(200, 512), n...  5.31 us
    pallas_call x1, Pallas kernels, shards(): pl.pallas_call(far_kernel, out_shape=(f32(*state), f32(*state), f32(2, 32...  3.53 us
    ppermute x1, starting transfers between devices, shards(): other = lax.ppermute(got, 'co', swap)  3.36 us
    pallas_call x1, Pallas kernels, shards(): pl.pallas_call(near_kernel, out_shape=(f32(*state), f32(*state)), in_spec...  2.79 us
    ppermute x1, starting transfers between devices, shards(): other = lax.ppermute(other, 'co', swap)  1.46 us
    pallas_call x1, Pallas kernels, shards(): pl.pallas_call(columns_kernel, out_shape=near(N, 128), in_specs=[VMEM] *...  1.4 us
    ppermute x1, waiting for transfers between devices, shards(): other = lax.ppermute(other, 'co', swap)  1.37 us
  transfers between devices with their start and end apart: 2, of which 1 were waited for; matrix products, arithmetic and copies ran while one was open for 0% of the time, Pallas kernels for 5%

profile of v4, /device:TPU:1, one launch (start us, length us, event | category | flops | bytes accessed | tf_op | source)
XLA Modules:
  0.0 59.0 jit_solution(3731191854968000547)
XLA Ops:
  0.6 0.0 copy-start.1
  0.6 0.0 copy-start.2
  0.7 0.0 copy-start.4
  0.7 0.0 copy-start.5
  0.7 5.3 %front.1 = (f32[200,512]{1,0:T(8,128)S(1)}, f32[200,512]{1,0:T(8,128)S(1)}, f32[256,128]{1,0:T(8,128)S(1)}, f32[2,16,32,1024]{3,2,1,0:T(8,128)S(1)}, f32[2,16,32...) custom-call(f32[16]{0:T(128)} %doppler_hbm.1, f32[16]{0:T(128)} %weight_hbm.1, ...), custom_call_target="tpu_custom_call" | custom-call | tf_op jit(solution)/shard_map/front/pallas_call | solution.py:433
  6.0 1.5 %collective-permute-start = (f32[200,512]{1,0:T(8,128)S(1)}, f32[200,512]{1,0:T(8,128)S(1)}, u32[]{:S(2)}, u32[]{:S(2)}) collective-permute-start(f32[200,512]{1,0:T(8,128)S(1)} %get-tuple-element.19), channel_id=1, source_target_pairs={{0,1},{1,0},{2,3},{3,2},{4,5},{5,4},{6,7},{7,6},{8,9},{9,8},{10,11... | collective-permute-start | bytes 1228808 | tf_op jit(solution)/shard_map/ppermute | solution.py:449
  7.5 1.4 %collective-permute-done.other = f32[200,512]{1,0:T(8,128)S(1)} collective-permute-done((f32[200,512]{1,0:T(8,128)S(1)}, f32[200,512]{1,0:T(8,128)S(1)}, u32[]{:S(2)}, u32[]{:S(2)}) %collective-permute-start) | collective-permute-done | bytes 409632 | tf_op jit(solution)/shard_map/ppermute | solution.py:449
  8.8 0.2 pack.1
  9.0 23.5 %all_to_all.10 = f32[64,17,1,128]{3,2,1,0:T(1,128)S(1)} all-to-all(f32[64,17,1,128]{3,2,1,0:T(1,128)S(1)} %bitcast.10), channel_id=1, replica_groups=mesh['space'=32,'yh'=2,'co'=2] {'space','yh'}, dimensions={0} | all-to-all | bytes 1114112 | tf_op jit(solution)/shard_map/all_to_all | solution.py:461
  32.5 0.0 copy-done.1
  32.5 0.0 copy-done.2
  32.5 0.0 copy-done.4
  32.5 0.0 copy-done.5
  32.5 1.4 %columns.1 = f32[1024,128]{1,0:T(8,128)S(1)} custom-call(f32[1088,128]{1,0:T(8,128)S(1)} %bitcast.9, bf16[2,256,256]{2,1,0:T(8,128)(2,1)S(1)} %copy-done.2, bf16[2,256,256]{2,1,0:T(8,128)(2,1)S(1)} %copy-done.1, f32[2,32,128]{2,1,0:T(8,128)S(1)} %copy-done.5, f32[2,32,128]{2,1,0:T(8,128)S(1)} %copy-done.4), custom_call_target="tpu_custom_call" | custom-call | tf_op jit(solution)/shard_map/columns/pallas_call | solution.py:465
  33.9 15.3 %all_to_all.11 = f32[64,16,1,128]{3,1,2,0:T(8,128)S(1)} all-to-all(f32[64,16,1,128]{3,1,2,0:T(8,128)S(1)} %bitcast.11), channel_id=1, replica_groups=mesh['space'=32,'yh'=2,'co'=2] {'space','yh'}, dimensions={0} | all-to-all | bytes 1048576 | tf_op jit(solution)/shard_map/all_to_all | solution.py:461
  49.2 3.4 %collective-permute-start.1 = (f32[1024,128]{1,0:T(8,128)S(1)}, f32[1024,128]{1,0:T(8,128)S(1)}, u32[]{:S(2)}, u32[]{:S(2)}) collective-permute-start(f32[1024,128]{1,0:T(8,128)S(1)} %bitcast.6), channel_id=1, source_target_pairs={{0,1},{1,0},{2,3},{3,2},{4,5},{5,4},{6,7},{7,6},{8,9},{9,8},{10,11... | collective-permute-start | bytes 1572872 | tf_op jit(solution)/shard_map/ppermute | solution.py:474
  52.6 0.0 copy-start
  52.6 0.0 copy-start.3
  52.6 0.0 copy-start.6
  52.6 0.0 copy-start.7
  52.6 2.8 %near.1 = (f32[2,16,32,1024]{3,2,1,0:T(8,128)}, f32[2,16,32,1024]{3,2,1,0:T(8,128)}) custom-call(f32[48,8,128]{2,1,0:T(8,128)S(1)} %get-tuple-element.17.rates, f32[1024,128]{1,0:T(8,128)S(1)} %bitcast.7, f32[2,16,32,1024]{3,2,1,0:T(8,128)S(1)} %get-tuple-element.21.a, f32[2,16,32,1024]{3,2,1,0:T(8,128)S(1)} %get-tuple-element.22.b, ...), custom_call_target="tpu_custom_call" | custom-call | tf_op jit(solution)/shard_map/near/pallas_call | solution.py:481
  55.4 0.0 collective-permute-done.1.other
  55.4 0.0 copy-done
  55.4 0.0 copy-done.3
  55.5 0.0 copy-done.6
  55.5 0.0 copy-done.7
  55.5 3.5 %far.1 = (f32[2,16,32,1024]{3,2,1,0:T(8,128)}, f32[2,16,32,1024]{3,2,1,0:T(8,128)}, f32[2,32,1024]{2,1,0:T(8,128)}, f32[2,32,1024]{2,1,0:T(8,128)}) custom-call(f32[48,8,128]{2,1,0:T(8,128)S(1)} %get-tuple-element.17.rates, f32[1024,128]{1,0:T(8,128)S(1)} %bitcast.8, ...), custom_call_target="tpu_custom_call", output_to_operand_aliasing={{0}: (10, {}), {1}: (11, {})} | custom-call | tf_op jit(solution)/shard_map/far/pallas_call | solution.py:491
Async XLA Ops:
  0.6 31.9 %copy-start.1 = (bf16[2,256,256]{2,1,0:T(8,128)(2,1)S(1)}, bf16[2,256,256]{2,1,0:T(8,128)(2,1)}, u32[]{:S(2)}) copy-start(bf16[2,256,256]{2,1,0:T(8,128)(2,1)} %constant.27.clone.left) | copy-start | bytes 786436
  0.6 31.8 %copy-start.2 = (bf16[2,256,256]{2,1,0:T(8,128)(2,1)S(1)}, bf16[2,256,256]{2,1,0:T(8,128)(2,1)}, u32[]{:S(2)}) copy-start(bf16[2,256,256]{2,1,0:T(8,128)(2,1)} %constant.26.clone.right) | copy-start | bytes 786436
  0.7 31.8 %copy-start.4 = (f32[2,32,128]{2,1,0:T(8,128)S(1)}, f32[2,32,128]{2,1,0:T(8,128)}, u32[]{:S(2)}) copy-start(f32[2,32,128]{2,1,0:T(8,128)} %constant.29.clone.wave) | copy-start | bytes 98308
  0.7 31.8 %copy-start.5 = (f32[2,32,128]{2,1,0:T(8,128)S(1)}, f32[2,32,128]{2,1,0:T(8,128)}, u32[]{:S(2)}) copy-start(f32[2,32,128]{2,1,0:T(8,128)} %constant.28.clone.twiddle) | copy-start | bytes 98308
  6.0 2.8 %collective-permute-start = (f32[200,512]{1,0:T(8,128)S(1)}, f32[200,512]{1,0:T(8,128)S(1)}, u32[]{:S(2)}, u32[]{:S(2)}) collective-permute-start(f32[200,512]{1,0:T(8,128)S(1)} %get-tuple-element.19), channel_id=1, source_target_pairs={{0,1},{1,0},{2,3},{3,2},{4,5},{5,4},{6,7},{7,6},{8,9},{9,8},{10,11... | collective-permute-start | bytes 1228808 | tf_op jit(solution)/shard_map/ppermute | solution.py:449
  49.2 6.2 %collective-permute-start.1 = (f32[1024,128]{1,0:T(8,128)S(1)}, f32[1024,128]{1,0:T(8,128)S(1)}, u32[]{:S(2)}, u32[]{:S(2)}) collective-permute-start(f32[1024,128]{1,0:T(8,128)S(1)} %bitcast.6), channel_id=1, source_target_pairs={{0,1},{1,0},{2,3},{3,2},{4,5},{5,4},{6,7},{7,6},{8,9},{9,8},{10,11... | collective-permute-start | bytes 1572872 | tf_op jit(solution)/shard_map/ppermute | solution.py:474
  52.6 2.8 %copy-start = (bf16[2,256,512]{2,1,0:T(8,128)(2,1)S(1)}, bf16[2,256,512]{2,1,0:T(8,128)(2,1)}, u32[]{:S(2)}) copy-start(bf16[2,256,512]{2,1,0:T(8,128)(2,1)} %constant.31.clone.table) | copy-start | bytes 1572868
  52.6 2.8 %copy-start.3 = (f32[8,256]{1,0:T(8,128)S(1)}, f32[8,256]{1,0:T(8,128)}, u32[]{:S(2)}) copy-start(f32[8,256]{1,0:T(8,128)} %constant.23.clone.twiddle_hbm.twiddle) | copy-start | bytes 24580
  52.6 2.8 %copy-start.6 = (f32[2,1024]{1,0:T(2,128)S(1)}, f32[2,1024]{1,0:T(2,128)}, u32[]{:S(2)}) copy-start(f32[2,1024]{1,0:T(2,128)} %constant.32.clone.post) | copy-start | bytes 24580
  52.6 2.8 %copy-start.7 = (f32[8,256]{1,0:T(8,128)S(1)}, f32[8,256]{1,0:T(8,128)}, u32[]{:S(2)}) copy-start(f32[8,256]{1,0:T(8,128)} %constant.30.clone.pre) | copy-start | bytes 24580
